TPU v7x, 256 devices: a whole 4x4x8 slice. The times are simulated.
256 devices in a mesh: circ: 64 (over x_lo, y, z), span: 4 (over x_hi, core).
Axes of the slice: x: 4 (x_hi: 2, x_lo: 2; x = x_hi * 2 + x_lo), y: 4, z: 8, core: 2. Of those that a mesh axis runs over, the one named last changes fastest.
Arguments:
- coefficients: float32 [65, 5, 16, 4096], P(None, None, 'span', 'circ'), may hold values from -3 to 3
- local_step: float32 [16, 2048, 256], P('span', 'circ'), may hold values from 0.1 to 0.4
- jacobian: float32 [3, 5, 5], replicated, may hold values from -2.5 to 2.5
- harmonic_numbers: int32 [32], replicated, may hold values from 1 to 64
- nodal_diameter: int32 [1], replicated, may hold values from 1 to 64
Outputs:
- new_state: float32 [5, 16, 2048, 256], P(None, 'span', 'circ')
All inputs are finite; a program needn't handle non-finite values.
Results may differ from a plain program's by a relative error of at most 0.0001.
Values sent between devices are 32-bit elements; how exact they have to be, the bound alone decides.
No kernel may reach another device: no remote copies, remote signals or barrier semaphores. Data moves between devices by JAX's collectives and lax.ppermute only.
A program may use at most 128 MiB of HBM per device.

v0:
```python
import math

import jax
import jax.numpy as jnp
from jax import lax
from jax.sharding import PartitionSpec as P

VARS = 5
PASS_DEV = 2
PITCH = 16
AXIAL = 256


section_weight = 0.5
dissipation = 0.125


def extended(array, sides, width, wrap):
    for axis, dim in sides:
        count, length = (lax.axis_size(axis), array.shape[dim])
        up = [(i, (i + 1) % count) for i in range(count if wrap else count - 1)]
        down = [(j, i) for i, j in up]
        last = lax.slice_in_dim(array, length - width, length, axis=dim)
        initial = lax.slice_in_dim(array, 0, width, axis=dim)
        before = lax.ppermute(last, axis, up)
        after = lax.ppermute(initial, axis, down)
        array = jnp.concatenate([before, array, after], axis=dim)
    return array


def phase_table(harmonic_numbers, nodal_diameter, passages, cycle_count):
    phase_turn = harmonic_numbers[None, :] * nodal_diameter[0] % cycle_count
    phase_turn = phase_turn * passages[:, None] % cycle_count
    phase_angle = phase_turn.astype(jnp.float32) * jnp.float32(2.0 * math.pi / cycle_count)
    mean_column = jnp.ones((passages.shape[0], 1), jnp.float32)
    return jnp.concatenate([mean_column, jnp.cos(phase_angle), jnp.sin(phase_angle)], axis=1)


def section_update(flow_state, span_pad, pitch_pad, jacobian, local_step):
    axial_pad = jnp.pad(flow_state, ((0, 0), (0, 0), (0, 0), (1, 1)))
    neighbours = [
        (span_pad[:, 2:], span_pad[:, :-2]),
        (pitch_pad[:, :, 2:], pitch_pad[:, :, :-2]),
        (axial_pad[:, :, :, 2:], axial_pad[:, :, :, :-2]),
    ]
    resid = jnp.zeros(flow_state.shape, jnp.float32)
    for direction in range(3):
        plus_side, minus_side = neighbours[direction]
        flux_part = jnp.einsum(
            "vw,wsqa->vsqa",
            jacobian[direction],
            0.5 * (plus_side - minus_side),
            precision=lax.Precision.HIGHEST,
        )
        resid = resid + flux_part - dissipation * (plus_side - 2.0 * flow_state + minus_side)
    return flow_state - section_weight * local_step[None] * resid


def send_rims(flow_state):
    return extended(flow_state, (("circ", 2),), 1, True)


def local(coefficients, local_step, jacobian, harmonic_numbers, nodal_diameter):
    layers = coefficients.shape[2]
    cycle_size = lax.axis_size("circ")
    passages_all = PASS_DEV * cycle_size
    first_pass = lax.axis_index("circ") * PASS_DEV
    extra = 0
    owned = (first_pass - extra // 2 + jnp.arange(PASS_DEV + extra, dtype=jnp.int32)) % passages_all
    phases = phase_table(harmonic_numbers, nodal_diameter, owned, passages_all)
    fields = jnp.einsum(
        "pi,ivsc->pvsc",
        phases,
        lax.all_gather(coefficients, "circ", axis=3, tiled=True),
        precision=lax.Precision.HIGHEST,
    )
    fields = fields.reshape(PASS_DEV + extra, VARS, layers, PITCH, AXIAL)
    flow_state = fields.transpose(1, 2, 0, 3, 4).reshape(VARS, layers, PASS_DEV * PITCH, AXIAL)
    pitch_pad = send_rims(flow_state)
    span_pad = extended(flow_state, (("span", 1),), 1, False)
    return section_update(flow_state, span_pad, pitch_pad, jacobian, local_step)


def solution(mesh):
    in_specs = (P(None, None, "span", "circ"), P("span", "circ", None), P(), P(), P())
    out_specs = P(None, "span", "circ", None)
    return jax.shard_map(local, mesh=mesh, in_specs=in_specs, out_specs=out_specs, check_vma=False)
```

profile of v0, /device:TPU:1, one launch (start us, length us, event | category | flops | bytes accessed | tf_op | source)
XLA Modules:
  0.0 546.3 jit_solution(13596435359046372487)
XLA Ops:
  6.5 0.0 all-gather.2.cloned.1.call-start
  6.5 0.7 all-gather.2.cloned.1.call-update
  7.9 0.7 and_select_fusion.2
  8.6 0.1 fusion.29
  8.7 0.8 fusion.39
  9.5 0.9 broadcast_multiply_fusion
  10.5 465.5 %all-gather.2.cloned.1.call-done = f32[65,5,4,4096]{0,3,2,1:T(8,128)} async-done(((f32[65,5,4,64]{0,3,2,1:T(8,128)}), f32[65,5,4,4096]{0,3,2,1:T(8,128)}) %all-gather.2.cloned.1.call-update) | async-done | bytes 21299216 | tf_op jit(solution)/shard_map/all_gather | solution.py:74
  476.0 38.7 %fusion.21 = f32[2,5,4,4096]{3,0,2,1:T(2,128)S(1)} fusion(f32[65,5,4,4096]{0,3,2,1:T(8,128)} %all-gather.2.cloned.1.call-done, f32[2,32]{1,0:T(2,128)S(1)} %get-tuple-element.13, f32[2,32]{1,0:T(2,128)S(1)} %get-tuple-element.12, f32[65]{0:T(128)S(1)} %pad.13.clone), kind=kOutput, calls=%fused_computation.46 | convolution fusion | flops 127795456 | bytes 21955332 | tf_op jit(solution)/shard_map/pi,ivsc->pvsc/dot_general | solution.py:71
  514.7 0.6 reshape.31
  515.3 0.4 copy.6
  515.8 0.1 collective-permute-start.3
  515.9 5.7 %collective-permute-start.2 = (f32[5,4,1,256]{3,0,2,1:T(8,128)S(1)}, f32[5,4,1,256]{3,0,2,1:T(8,128)S(1)}, u32[]{:S(2)}, u32[]{:S(2)}) collective-permute-start(f32[5,4,1,256]{3,0,2,1:T(8,128)S(1)} %get-tuple-element.8), channel_id=1, source_target_pairs={{4,0},{8,4},{12,8},{16,12},{20,16},{24,20},{28,24},{32,28},{36,32}... | collective-permute-start | bytes 61448 | tf_op jit(solution)/shard_map/ppermute | solution.py:26
  521.5 5.6 %collective-permute-start.1 = (f32[5,1,32,256]{3,0,2,1:T(8,128)S(1)}, f32[5,1,32,256]{3,0,2,1:T(8,128)S(1)}, u32[]{:S(2)}, u32[]{:S(2)}) collective-permute-start(f32[5,1,32,256]{3,0,2,1:T(8,128)S(1)} %get-tuple-element.5), channel_id=1, source_target_pairs={{0,1},{1,2},{2,3},{4,5},{5,6},{6,7},{8,9},{9,10},{10,11},{12,13},{... | collective-permute-start | bytes 491528 | tf_op jit(solution)/shard_map/ppermute | solution.py:25
  527.1 2.1 collective-permute-start
  529.2 1.4 convolution_bitcast_fusion
  530.7 0.0 collective-permute-done.3
  530.7 0.0 collective-permute-done.2
  530.7 1.1 convolution_bitcast_fusion.1
  531.8 0.0 collective-permute-done.1
  531.8 4.5 collective-permute-done
  536.3 2.0 fusion.6
  538.4 1.0 copy.10
  (4 shorter events, 0.1 us)
Async XLA Ops:
  6.5 469.5 %all-gather.2.cloned.1.call-start = ((), (), s32[]{:S(2)}) async-start(), calls=%async_computation | async-start | bytes 42598400 | tf_op jit(solution)/shard_map/all_gather | solution.py:74
  515.8 14.9 %collective-permute-start.3 = (f32[5,4,1,256]{3,0,2,1:T(8,128)S(1)}, f32[5,4,1,256]{3,0,2,1:T(8,128)S(1)}, u32[]{:S(2)}, u32[]{:S(2)}) collective-permute-start(f32[5,4,1,256]{3,0,2,1:T(8,128)S(1)} %get-tuple-element.7), channel_id=1, source_target_pairs={{0,4},{4,8},{8,12},{12,16},{16,20},{20,24},{24,28},{28,32},{32,36}... | collective-permute-start | bytes 61448 | tf_op jit(solution)/shard_map/ppermute | solution.py:25
  515.9 14.8 %collective-permute-start.2 = (f32[5,4,1,256]{3,0,2,1:T(8,128)S(1)}, f32[5,4,1,256]{3,0,2,1:T(8,128)S(1)}, u32[]{:S(2)}, u32[]{:S(2)}) collective-permute-start(f32[5,4,1,256]{3,0,2,1:T(8,128)S(1)} %get-tuple-element.8), channel_id=1, source_target_pairs={{4,0},{8,4},{12,8},{16,12},{20,16},{24,20},{28,24},{32,28},{36,32}... | collective-permute-start | bytes 61448 | tf_op jit(solution)/shard_map/ppermute | solution.py:26
  521.5 10.3 %collective-permute-start.1 = (f32[5,1,32,256]{3,0,2,1:T(8,128)S(1)}, f32[5,1,32,256]{3,0,2,1:T(8,128)S(1)}, u32[]{:S(2)}, u32[]{:S(2)}) collective-permute-start(f32[5,1,32,256]{3,0,2,1:T(8,128)S(1)} %get-tuple-element.5), channel_id=1, source_target_pairs={{0,1},{1,2},{2,3},{4,5},{5,6},{6,7},{8,9},{9,10},{10,11},{12,13},{... | collective-permute-start | bytes 491528 | tf_op jit(solution)/shard_map/ppermute | solution.py:25
  527.1 9.2 %collective-permute-start = (f32[5,1,32,256]{3,0,2,1:T(8,128)S(1)}, f32[5,1,32,256]{3,0,2,1:T(8,128)S(1)}, u32[]{:S(2)}, u32[]{:S(2)}) collective-permute-start(f32[5,1,32,256]{3,0,2,1:T(8,128)S(1)} %get-tuple-element.6), channel_id=1, source_target_pairs={{1,0},{2,1},{3,2},{5,4},{6,5},{7,6},{9,8},{10,9},{11,10},{13,12},{... | collective-permute-start | bytes 491528 | tf_op jit(solution)/shard_map/ppermute | solution.py:26
Sparse Core Ops, SparseCore 0:
  9.1 466.8 all-gather.1
where the time goes:
time: 547 us; the launch traced here: 546 us
  waiting for transfers between devices  471 us (86%)
  matrix products  43.3 us (8%)
  between operations  14.2 us (3%)
  starting transfers between devices  13.4 us (2%)
    all_gather x1, waiting for transfers between devices, local(): lax.all_gather(coefficients, 'circ', axis=3, tiled=True)  466 us
    dot_general x1, matrix products, local(): jnp.einsum('pi,ivsc->pvsc', phases, lax.all_gather(coefficients, 'circ',...  38.7 us
  transfers between devices with their start and end apart: 5, of which 2 were waited for; matrix products, arithmetic and copies ran while one was open for 1% of the time, Pallas kernels for 0%

commit v1 on v0

v1 whole, which is shorter than its diff:
```python
import jax, jax.numpy as jnp
from jax import lax
from jax.sharding import PartitionSpec as P
import math

def phase_table(h, nd, passages, n):
    t = h[None, :] * nd[0] % n
    t = t * passages[:, None] % n
    ang = t.astype(jnp.float32) * jnp.float32(2.0 * math.pi / n)
    return jnp.concatenate([jnp.ones((passages.shape[0], 1), jnp.float32), jnp.cos(ang), jnp.sin(ang)], axis=1)

def extended(array, sides, width, wrap):
    for axis, dim in sides:
        count, length = (lax.axis_size(axis), array.shape[dim])
        up = [(i, (i + 1) % count) for i in range(count if wrap else count - 1)]
        down = [(j, i) for i, j in up]
        last = lax.slice_in_dim(array, length - width, length, axis=dim)
        initial = lax.slice_in_dim(array, 0, width, axis=dim)
        before = lax.ppermute(last, axis, up)
        after = lax.ppermute(initial, axis, down)
        array = jnp.concatenate([before, array, after], axis=dim)
    return array

def section_update(flow_state, span_pad, pitch_pad, jacobian, local_step):
    axial_pad = jnp.pad(flow_state, ((0, 0), (0, 0), (0, 0), (1, 1)))
    neighbours = [
        (span_pad[:, 2:], span_pad[:, :-2]),
        (pitch_pad[:, :, 2:], pitch_pad[:, :, :-2]),
        (axial_pad[:, :, :, 2:], axial_pad[:, :, :, :-2]),
    ]
    resid = jnp.zeros(flow_state.shape, jnp.float32)
    for direction in range(3):
        p, m = neighbours[direction]
        f = jnp.einsum("vw,wsqa->vsqa", jacobian[direction], 0.5 * (p - m), precision=lax.Precision.HIGHEST)
        resid = resid + f - 0.125 * (p - 2.0 * flow_state + m)
    return flow_state - 0.5 * local_step[None] * resid

def local(coefficients, local_step, jacobian, harmonic_numbers, nodal_diameter):
    phases = phase_table(harmonic_numbers, nodal_diameter, jnp.arange(128, dtype=jnp.int32), 128)
    f = jnp.einsum("pi,ivk->pvk", phases, coefficients.reshape(65, 5, 256), precision=lax.Precision.HIGHEST)
    f = f.reshape(64, 2, 5, 2, 128).transpose(0, 2, 1, 3, 4).reshape(64, 5, 4, 128)
    r = lax.all_to_all(f, "circ", 0, 0, tiled=True)
    r = r.reshape(16, 4, 5, 2, 2, 2, 64)
    flow = r.transpose(2, 4, 5, 3, 0, 1, 6).reshape(5, 4, 32, 256)
    pitch_pad = extended(flow, (("circ", 2),), 1, True)
    span_pad = extended(flow, (("span", 1),), 1, False)
    return section_update(flow, span_pad, pitch_pad, jacobian, local_step)

def solution(mesh):
    in_specs = (P(None, None, "span", "circ"), P("span", "circ", None), P(), P(), P())
    return jax.shard_map(local, mesh=mesh, in_specs=in_specs, out_specs=P(None, "span", "circ", None), check_vma=False)
```

time: 547 us -> 65.7 us (0.12)
  waiting for transfers between devices: 471 us -> 24.2 us
  matrix products: 43.3 us -> 5.31 us
  starting transfers between devices: 13.4 us -> 28.9 us
  between operations: 14.2 us -> 0.88 us
    all_gather x1 -> x0, waiting for transfers between devices: 466 us -> none  [local(): lax.all_gather(coefficients, 'circ', axis=3, tiled=True)]
    dot_general x4, matrix products: 43.3 us -> 5.31 us  [the longest x3 4.58 us: section_update(): jnp.einsum('vw,wsqa->vsqa', jacobian[direction], 0.5 * (p - m), precision...]
    all_to_all x0 -> x1, waiting for transfers between devices: none -> 19.5 us  [local(): r = lax.all_to_all(f, 'circ', 0, 0, tiled=True)]
    all_to_all x0 -> x1, starting transfers between devices: none -> 13.6 us  [local(): r = lax.all_to_all(f, 'circ', 0, 0, tiled=True)]
  transfers between devices with their start and end apart: 5 -> 5, of which waited for: 2 -> 2; matrix products, arithmetic and copies ran while one was open for 1% -> 4% of each run, Pallas kernels for 0% -> 0%
where the time goes in v1:
time: 65.7 us; the launch traced here: 65.5 us
  starting transfers between devices  28.9 us (44%)
  waiting for transfers between devices  24.2 us (37%)
  local copies, waits for them, and re-layouts  5.84 us (9%)
  matrix products  5.31 us (8%)
  between operations  0.88 us (1%)
    all_to_all x1, waiting for transfers between devices, local(): r = lax.all_to_all(f, 'circ', 0, 0, tiled=True)  19.5 us
    all_to_all x1, starting transfers between devices, local(): r = lax.all_to_all(f, 'circ', 0, 0, tiled=True)  13.6 us
    ppermute x2, starting transfers between devices, extended(): before = lax.ppermute(last, axis, up)  9.12 us
    ppermute x2, starting transfers between devices, extended(): after = lax.ppermute(initial, axis, down)  6.22 us
    ppermute x2, waiting for transfers between devices, extended(): after = lax.ppermute(initial, axis, down)  4.69 us
    dot_general x3, matrix products, section_update(): jnp.einsum('vw,wsqa->vsqa', jacobian[direction], 0.5 * (p - m), precision...  4.58 us
    reshape x1, local copies, waits for them, and re-layouts, local(): coefficients.reshape(65, 5, 256)  1.34 us
  transfers between devices with their start and end apart: 5, of which 2 were waited for; matrix products, arithmetic and copies ran while one was open for 4% of the time, Pallas kernels for 0%

profile of v1, /device:TPU:1, one launch (start us, length us, event | category | flops | bytes accessed | tf_op | source)
XLA Modules:
  0.0 65.5 jit_solution(2697708093597067218)
XLA Ops:
  0.0 0.0 copy-start.2
  0.7 1.3 %copy.29 = f32[65,5,256]{2,0,1:T(8,128)S(1)} copy(f32[65,5,256]{0,2,1:T(8,128)} %bitcast.69) | data formatting | bytes 665600 | tf_op jit(solution)/shard_map/reshape | solution.py:40
  2.0 0.2 dot_general.23
  2.2 0.0 copy-done.2
  2.2 0.3 fusion.28
  2.6 0.7 %convolution_bitcast_fusion.3 = f32[64,5,2,2,128]{4,0,3,1,2:T(8,128)S(1)} fusion(f32[5,2,128,65]{2,1,3,0:T(2,128)S(1)} %dot_general.23, f32[64,2,32]{2,0,1:T(8,128)S(1)} %get-tuple-element.13, f32[64,2,32]{2,0,1:T(8,128)S(1)} %get-tuple-element.12, f32[65]{0:T(128)S(1)} %pad.13.clone), kind=kOutput, calls=%fused_computation.12 | convolution fusion | flops 127811840 | bytes 1021188 | tf_op jit(solution)/shard_map/pi,ivk->pvk/dot_general | solution.py:40
  3.4 0.0 copy-start.1
  3.4 0.0 copy-start
  3.4 1.3 %copy.32 = f32[64,5,4,128]{3,2,1,0:T(4,128)} copy(f32[64,5,4,128]{3,0,2,1:T(8,128)S(1)} %bitcast.67) | data formatting | bytes 1310720 | tf_op jit(solution)/shard_map/reshape | solution.py:41
  4.6 13.6 %all-to-all-start = ((f32[64,5,4,128]{3,2,1,0:T(4,128)}), f32[64,5,4,128]{3,2,1,0:T(4,128)S(1)}, u32[]{:S(2)}, u32[]{:S(2)}) async-start(f32[64,5,4,128]{3,2,1,0:T(4,128)} %copy.32), calls=%async_computation | async-start | bytes 1310720 | tf_op jit(solution)/shard_map/all_to_all | solution.py:42
  18.2 0.0 copy-done.1
  18.2 0.0 copy-done
  18.3 19.5 %all-to-all-done = f32[64,5,4,128]{3,2,1,0:T(4,128)S(1)} async-done(((f32[64,5,4,128]{3,2,1,0:T(4,128)}), f32[64,5,4,128]{3,2,1,0:T(4,128)S(1)}, u32[]{:S(2)}, u32[]{:S(2)}) %all-to-all-start) | async-done | bytes 655392 | tf_op jit(solution)/shard_map/all_to_all | solution.py:42
  37.8 0.1 copy.33
  37.9 0.8 %reshape.51 = f32[16,4,5,2,2,2,64]{6,5,1,0,4,3,2:T(2,128)S(1)} reshape(f32[64,5,4,128]{3,0,2,1:T(8,128)S(1)} %copy.33) | data formatting | bytes 1310720 | tf_op jit(solution)/shard_map/reshape | solution.py:43
  38.6 0.3 copy.54
  39.0 0.8 %reshape.58 = f32[5,4,32,256]{3,0,2,1:T(8,128)S(1)} reshape(f32[5,2,2,2,16,4,64]{6,5,0,4,3,2,1:T(4,128)S(1)} %copy.54) | data formatting | bytes 1310720 | tf_op jit(solution)/shard_map/reshape | solution.py:44
  39.8 1.5 %collective-permute-start.3 = (f32[5,4,1,256]{3,0,2,1:T(8,128)S(1)}, f32[5,4,1,256]{3,0,2,1:T(8,128)S(1)}, u32[]{:S(2)}, u32[]{:S(2)}) collective-permute-start(f32[5,4,1,256]{3,0,2,1:T(8,128)S(1)} %get-tuple-element.7), channel_id=1, source_target_pairs={{0,4},{4,8},{8,12},{12,16},{16,20},{20,24},{24,28},{28,32},{32,36}... | collective-permute-start | bytes 61448 | tf_op jit(solution)/shard_map/ppermute | solution.py:19
  41.2 4.3 %collective-permute-start.2 = (f32[5,4,1,256]{3,0,2,1:T(8,128)S(1)}, f32[5,4,1,256]{3,0,2,1:T(8,128)S(1)}, u32[]{:S(2)}, u32[]{:S(2)}) collective-permute-start(f32[5,4,1,256]{3,0,2,1:T(8,128)S(1)} %get-tuple-element.8), channel_id=1, source_target_pairs={{4,0},{8,4},{12,8},{16,12},{20,16},{24,20},{28,24},{32,28},{36,32}... | collective-permute-start | bytes 61448 | tf_op jit(solution)/shard_map/ppermute | solution.py:20
  45.5 7.7 %collective-permute-start.1 = (f32[5,1,32,256]{3,0,2,1:T(8,128)S(1)}, f32[5,1,32,256]{3,0,2,1:T(8,128)S(1)}, u32[]{:S(2)}, u32[]{:S(2)}) collective-permute-start(f32[5,1,32,256]{3,0,2,1:T(8,128)S(1)} %get-tuple-element.5), channel_id=1, source_target_pairs={{0,1},{1,2},{2,3},{4,5},{5,6},{6,7},{8,9},{9,10},{10,11},{12,13},{... | collective-permute-start | bytes 491528 | tf_op jit(solution)/shard_map/ppermute | solution.py:19
  53.2 1.9 %collective-permute-start = (f32[5,1,32,256]{3,0,2,1:T(8,128)S(1)}, f32[5,1,32,256]{3,0,2,1:T(8,128)S(1)}, u32[]{:S(2)}, u32[]{:S(2)}) collective-permute-start(f32[5,1,32,256]{3,0,2,1:T(8,128)S(1)} %get-tuple-element.6), channel_id=1, source_target_pairs={{1,0},{2,1},{3,2},{5,4},{6,5},{7,6},{9,8},{10,9},{11,10},{13,12},{... | collective-permute-start | bytes 491528 | tf_op jit(solution)/shard_map/ppermute | solution.py:20
  55.1 1.4 %convolution_bitcast_fusion = f32[5,4,32,256]{3,0,2,1:T(8,128)S(1)} fusion(f32[5,4,32,256]{3,0,2,1:T(8,128)S(1)} %reshape.58, f32[1,5,5]{2,0,1:T(1,128)S(1)} %get-tuple-element.11), kind=kOutput, calls=%fused_computation.2 | convolution fusion | flops 10158080 | bytes 1310820 | tf_op jit(solution)/shard_map/vw,wsqa->vsqa/dot_general | solution.py:34
  56.6 0.0 collective-permute-done.3
  56.6 0.0 collective-permute-done.2
  56.6 1.1 %convolution_bitcast_fusion.1 = f32[5,4,32,256]{3,0,2,1:T(8,128)S(1)} fusion(f32[5,4,1,256]{3,0,2,1:T(8,128)S(1)} %collective-permute-done.2, f32[5,4,32,256]{3,0,2,1:T(8,128)S(1)} %reshape.58, f32[5,4,1,256]{3,0,2,1:T(8,128)S(1)} %collective-permute-done.3, f32[1,5,5]{2,0,1:T(1,128)S(1)} %get-tuple-element.10), kind=kOutput, calls=%fused_computation.3 | convolution fusion | flops 10485760 | bytes 1351780 | tf_op jit(solution)/shard_map/vw,wsqa->vsqa/dot_general | solution.py:34
  57.7 0.0 collective-permute-done.1
  57.7 4.7 %collective-permute-done = f32[5,1,32,256]{3,0,2,1:T(8,128)S(1)} collective-permute-done((f32[5,1,32,256]{3,0,2,1:T(8,128)S(1)}, f32[5,1,32,256]{3,0,2,1:T(8,128)S(1)}, u32[]{:S(2)}, u32[]{:S(2)}) %collective-permute-start) | collective-permute-done | bytes 163872 | tf_op jit(solution)/shard_map/ppermute | solution.py:20
  62.4 2.0 %fusion.6 = f32[5,4,32,256]{3,0,2,1:T(8,128)S(1)} fusion(f32[5,4,32,256]{3,0,2,1:T(8,128)S(1)} %reshape.58, f32[5,4,32,256]{3,0,2,1:T(8,128)S(1)} %convolution_bitcast_fusion, f32[5,4,32,256]{3,0,2,1:T(8,128)S(1)} %convolution_bitcast_fusion.1, f32[5,1,32,256]{3,0,2,1:T(8,128)S(1)} %collective-permute-done, ...), kind=kOutput, calls=%fused_computation.11 | convolution fusion | flops 13926400 | bytes 6097408 | tf_op jit(solution)/shard_map/vw,wsqa->vsqa/dot_general | solution.py:34
  64.5 1.0 %copy.49 = f32[5,4,32,256]{3,2,1,0:T(8,128)} copy(f32[5,4,32,256]{3,0,2,1:T(8,128)S(1)} %fusion.6) | data formatting | bytes 1310720 | tf_op jit(solution)/shard_map/sub | solution.py:36
  (8 shorter events, 0.1 us)
Async XLA Ops:
  0.0 2.2 %copy-start.2 = (s32[32]{0:T(128)S(1)}, s32[32]{0:T(128)}, u32[]{:S(2)}) copy-start(s32[32]{0:T(128)} %param.8) | copy-start | bytes 388
  3.4 14.9 %copy-start.1 = (f32[3,5,5]{2,0,1:T(4,128)S(1)}, f32[3,5,5]{2,0,1:T(4,128)}, u32[]{:S(2)}) copy-start(f32[3,5,5]{2,0,1:T(4,128)} %param.7) | copy-start | bytes 904
  3.4 14.9 %copy-start = (f32[4,32,256]{2,1,0:T(8,128)S(1)}, f32[4,32,256]{2,1,0:T(8,128)}, u32[]{:S(2)}) copy-start(f32[4,32,256]{2,1,0:T(8,128)} %param.6) | copy-start | bytes 393220
  4.6 33.1 %all-to-all-start = ((f32[64,5,4,128]{3,2,1,0:T(4,128)}), f32[64,5,4,128]{3,2,1,0:T(4,128)S(1)}, u32[]{:S(2)}, u32[]{:S(2)}) async-start(f32[64,5,4,128]{3,2,1,0:T(4,128)} %copy.32), calls=%async_computation | async-start | bytes 1310720 | tf_op jit(solution)/shard_map/all_to_all | solution.py:42
  39.8 16.8 %collective-permute-start.3 = (f32[5,4,1,256]{3,0,2,1:T(8,128)S(1)}, f32[5,4,1,256]{3,0,2,1:T(8,128)S(1)}, u32[]{:S(2)}, u32[]{:S(2)}) collective-permute-start(f32[5,4,1,256]{3,0,2,1:T(8,128)S(1)} %get-tuple-element.7), channel_id=1, source_target_pairs={{0,4},{4,8},{8,12},{12,16},{16,20},{20,24},{24,28},{28,32},{32,36}... | collective-permute-start | bytes 61448 | tf_op jit(solution)/shard_map/ppermute | solution.py:19
  41.2 15.3 %collective-permute-start.2 = (f32[5,4,1,256]{3,0,2,1:T(8,128)S(1)}, f32[5,4,1,256]{3,0,2,1:T(8,128)S(1)}, u32[]{:S(2)}, u32[]{:S(2)}) collective-permute-start(f32[5,4,1,256]{3,0,2,1:T(8,128)S(1)} %get-tuple-element.8), channel_id=1, source_target_pairs={{4,0},{8,4},{12,8},{16,12},{20,16},{24,20},{28,24},{32,28},{36,32}... | collective-permute-start | bytes 61448 | tf_op jit(solution)/shard_map/ppermute | solution.py:20
  45.5 12.2 %collective-permute-start.1 = (f32[5,1,32,256]{3,0,2,1:T(8,128)S(1)}, f32[5,1,32,256]{3,0,2,1:T(8,128)S(1)}, u32[]{:S(2)}, u32[]{:S(2)}) collective-permute-start(f32[5,1,32,256]{3,0,2,1:T(8,128)S(1)} %get-tuple-element.5), channel_id=1, source_target_pairs={{0,1},{1,2},{2,3},{4,5},{5,6},{6,7},{8,9},{9,10},{10,11},{12,13},{... | collective-permute-start | bytes 491528 | tf_op jit(solution)/shard_map/ppermute | solution.py:19
  53.2 9.2 %collective-permute-start = (f32[5,1,32,256]{3,0,2,1:T(8,128)S(1)}, f32[5,1,32,256]{3,0,2,1:T(8,128)S(1)}, u32[]{:S(2)}, u32[]{:S(2)}) collective-permute-start(f32[5,1,32,256]{3,0,2,1:T(8,128)S(1)} %get-tuple-element.6), channel_id=1, source_target_pairs={{1,0},{2,1},{3,2},{5,4},{6,5},{7,6},{9,8},{10,9},{11,10},{13,12},{... | collective-permute-start | bytes 491528 | tf_op jit(solution)/shard_map/ppermute | solution.py:20

commit v2 on v1

v2 whole, which is shorter than its diff:
```python
import functools
import math

import jax
import jax.numpy as jnp
from jax import lax
from jax.experimental import pallas as pl
from jax.experimental.pallas import tpu as pltpu
from jax.sharding import PartitionSpec as P

VMEM = pl.BlockSpec(memory_space=pltpu.VMEM)
SMEM = pl.BlockSpec(memory_space=pltpu.SMEM)
F32 = jnp.float32
ROWS = 20


def cos_turns(index):
    folded = jnp.where(index > 64, 128 - index, index)
    flip = folded > 32
    quarter = jnp.where(flip, 64 - folded, folded).astype(F32) * F32(math.pi / 64)
    square = quarter * quarter
    terms = [1.0, -1.0 / 2, 1.0 / 24, -1.0 / 720, 1.0 / 40320, -1.0 / 3628800, 1.0 / 479001600, -1.0 / 87178291200]
    value = jnp.full(index.shape, terms[-1], F32)
    for term in terms[-2::-1]:
        value = value * square + F32(term)
    return jnp.where(flip, -value, value)


def expand_kernel(coef_ref, harm_ref, nodal_ref, out_ref):
    harm = jnp.concatenate([harm_ref[...], jnp.zeros((1, 96), jnp.int32)], axis=1)
    lane = lax.broadcasted_iota(jnp.int32, (8, 128), 1)[:1]
    turns = (pltpu.roll(harm, 1, 1) + pltpu.roll(harm, 33, 1)) * nodal_ref[0] & 127
    row = lax.broadcasted_iota(jnp.int32, (128, 128), 0)
    passage = jnp.where(row < 64, 2 * row, 2 * row - 127)
    index = turns * passage & 127
    index = jnp.where(lane > 32, index + 96 & 127, index)
    phases = cos_turns(index)[:, :65]
    for pair in range(10):
        block = lax.dot_general(
            phases,
            coef_ref[pair * 128 : pair * 128 + 128, :],
            (((1,), (1,)), ((), ())),
            precision=lax.Precision.HIGHEST,
            preferred_element_type=F32,
        )
        out_ref[pl.ds(pair, 64, ROWS), :] = block[:64]
        out_ref[pl.ds(pair + 10, 64, ROWS), :] = block[64:]


def gather_kernel(got_ref, parity_ref, flow_ref, inner_ref, outer_ref, first_ref, final_ref):
    low = lax.broadcasted_iota(jnp.int32, (16, 128), 1) < 64
    even = parity_ref[0] == 0
    for p in range(2):
        for v in range(5):
            for h in range(2):
                row = p * 10 + v * 2 + h
                parts = [got_ref[pl.ds(a * ROWS + row, 16, 4 * ROWS), :] for a in range(4)]
                turned = [pltpu.roll(x, 64, 1) for x in parts]
                for b in range(2):
                    cols = slice(128 * b, 128 * b + 128)
                    base = (v * 4 + 2 * h) * 32 + p * 16
                    flow_ref[base : base + 16, cols] = jnp.where(low, parts[2 * b], turned[2 * b + 1])
                    flow_ref[base + 32 : base + 48, cols] = jnp.where(low, turned[2 * b], parts[2 * b + 1])
    for v in range(5):
        bottom = flow_ref[v * 128 : v * 128 + 32, :]
        top = flow_ref[v * 128 + 96 : v * 128 + 128, :]
        inner_ref[v * 32 : v * 32 + 32, :] = jnp.where(even, top, bottom)
        outer_ref[v * 32 : v * 32 + 32, :] = jnp.where(even, bottom, top)
    for i in range(20):
        first_ref[i : i + 1, :] = flow_ref[i * 32 : i * 32 + 1, :]
        final_ref[i : i + 1, :] = flow_ref[i * 32 + 31 : i * 32 + 32, :]


def section_kernel(flow_ref, inner_ref, outer_ref, before_ref, after_ref, step_ref, jac_ref, parity_ref, out_ref):
    even = parity_ref[0] == 0
    row = lax.broadcasted_iota(jnp.int32, (8, 256), 0)
    lane = lax.broadcasted_iota(jnp.int32, (8, 256), 1)
    at_top, at_bottom = row == 0, row == 7
    at_left, at_right = lane == 0, lane == 255
    half = [[[0.5 * jac_ref[d, v, w] for w in range(5)] for v in range(5)] for d in range(3)]
    for s in range(4):
        for t in range(4):
            diffs, smooth = [], []
            for v in range(5):
                base = (v * 4 + s) * 32 + t * 8
                here = flow_ref[base : base + 8, :]
                side = slice(v * 32 + t * 8, v * 32 + t * 8 + 8)
                if s == 0:
                    s_minus = jnp.where(even, outer_ref[side, :], inner_ref[side, :])
                else:
                    s_minus = flow_ref[base - 32 : base - 24, :]
                if s == 3:
                    s_plus = jnp.where(even, inner_ref[side, :], outer_ref[side, :])
                else:
                    s_plus = flow_ref[base + 32 : base + 40, :]
                above = flow_ref[base - 1 : base, :] if t else before_ref[v * 4 + s : v * 4 + s + 1, :]
                below = flow_ref[base + 8 : base + 9, :] if t < 3 else after_ref[v * 4 + s : v * 4 + s + 1, :]
                p_minus = jnp.where(at_top, above, pltpu.roll(here, 1, 0))
                p_plus = jnp.where(at_bottom, below, pltpu.roll(here, 7, 0))
                a_minus = jnp.where(at_left, 0.0, pltpu.roll(here, 1, 1))
                a_plus = jnp.where(at_right, 0.0, pltpu.roll(here, 255, 1))
                diffs.append((s_plus - s_minus, p_plus - p_minus, a_plus - a_minus))
                total = (s_plus + s_minus) + (p_plus + p_minus) + (a_plus + a_minus)
                smooth.append((here, 0.75 * here - 0.125 * total))
            scale = 0.5 * step_ref[s * 32 + t * 8 : s * 32 + t * 8 + 8, :]
            for v in range(5):
                here, resid = smooth[v]
                for d in range(3):
                    for w in range(5):
                        resid = resid + half[d][v][w] * diffs[w][d]
                base = (v * 4 + s) * 32 + t * 8
                out_ref[base : base + 8, :] = here - scale * resid


def local(coefficients, local_step, jacobian, harmonic_numbers, nodal_diameter):
    shape = jax.ShapeDtypeStruct
    ring = lax.axis_size("circ")
    parity = (lax.axis_index("span") % 2).astype(jnp.int32).reshape(1)
    cells = coefficients.transpose(1, 2, 3, 0).reshape(1280, 65)
    sent = pl.pallas_call(
        expand_kernel,
        out_shape=shape((64 * ROWS, 128), F32),
        in_specs=[VMEM, VMEM, SMEM],
        out_specs=VMEM,
        name="expand",
        compiler_params=pltpu.CompilerParams(vmem_limit_bytes=8 << 20),
    )(cells, harmonic_numbers.reshape(1, 32), nodal_diameter)
    got = lax.all_to_all(sent.reshape(64, 5, 4, 128), "circ", 0, 0, tiled=True).reshape(64 * ROWS, 128)
    flow, inner, outer, first, final = pl.pallas_call(
        gather_kernel,
        out_shape=[shape((640, 256), F32), shape((160, 256), F32), shape((160, 256), F32), shape((20, 256), F32), shape((20, 256), F32)],
        in_specs=[VMEM, SMEM],
        out_specs=[VMEM] * 5,
        name="gather",
        compiler_params=pltpu.CompilerParams(vmem_limit_bytes=8 << 20),
    )(got, parity)
    outer = lax.ppermute(outer, "span", [(1, 2), (2, 1)])
    before = lax.ppermute(final, "circ", [(i, (i + 1) % ring) for i in range(ring)])
    after = lax.ppermute(first, "circ", [((i + 1) % ring, i) for i in range(ring)])
    inner = lax.ppermute(inner, "span", [(0, 1), (1, 0), (2, 3), (3, 2)])
    new = pl.pallas_call(
        section_kernel,
        out_shape=shape((640, 256), F32),
        in_specs=[VMEM] * 6 + [SMEM] * 2,
        out_specs=VMEM,
        name="section",
        compiler_params=pltpu.CompilerParams(vmem_limit_bytes=8 << 20),
    )(flow, inner, outer, before, after, local_step.reshape(128, 256), jacobian, parity)
    return new.reshape(5, 4, 32, 256)


def solution(mesh):
    in_specs = (P(None, None, "span", "circ"), P("span", "circ", None), P(), P(), P())
    out_specs = P(None, "span", "circ", None)
    return jax.shard_map(local, mesh=mesh, in_specs=in_specs, out_specs=out_specs, check_vma=False)
```

time: 65.7 us -> 55.5 us (0.84)
  Pallas kernels: 0 us -> 5.53 us
  matrix products: 5.31 us -> 0 us
  local copies, waits for them, and re-layouts: 5.84 us -> 1.74 us
  waiting for transfers between devices: 24.2 us -> 20.8 us
  starting transfers between devices: 28.9 us -> 26.6 us
    pallas_call x0 -> x3, Pallas kernels: none -> 5.53 us  [the longest x1 2.82 us: local(): pl.pallas_call(section_kernel, out_shape=shape((640, 256), F32), in_specs...]
    dot_general x4 -> x0, matrix products: 5.31 us -> none  [the longest x3 4.58 us: section_update(): jnp.einsum('vw,wsqa->vsqa', jacobian[direction], 0.5 * (p - m), precision...]
    reshape x5 -> x0, local copies, waits for them, and re-layouts: 4.44 us -> none  [the longest x1 1.34 us: local(): coefficients.reshape(65, 5, 256)]
    ppermute x4, waiting for transfers between devices: 4.69 us -> 1.21 us  [the longest x1 1.21 us: local(): lax.ppermute(final, 'circ', [(i, (i + 1) % ring) for i in range(ring)])]
    ppermute x4, starting transfers between devices: 15.3 us -> 13 us  [the longest x1 4.83 us: local(): lax.ppermute(first, 'circ', [((i + 1) % ring, i) for i in range(ring)])]
    unnamed x6 -> x9, local copies, waits for them, and re-layouts: 0.02 us -> 1.74 us
    sub x1 -> x0, local copies, waits for them, and re-layouts: 1.04 us -> none  [section_update(): return flow_state - 0.5 * local_step[None] * resid]
  transfers between devices with their start and end apart: 5 -> 5, of which waited for: 2 -> 2; matrix products, arithmetic and copies ran while one was open for 4% -> 0% of each run, Pallas kernels for 0% -> 0%
where the time goes in v2:
time: 55.5 us; the launch traced here: 55.3 us
  starting transfers between devices  26.6 us (48%)
  waiting for transfers between devices  20.8 us (37%)
  Pallas kernels  5.53 us (10%)
  local copies, waits for them, and re-layouts  1.74 us (3%)
  between operations  0.71 us (1%)
    all_to_all x1, waiting for transfers between devices, local(): lax.all_to_all(sent.reshape(64, 5, 4, 128), 'circ', 0, 0, tiled=True)  19.5 us
    all_to_all x1, starting transfers between devices, local(): lax.all_to_all(sent.reshape(64, 5, 4, 128), 'circ', 0, 0, tiled=True)  13.6 us
    ppermute x1, starting transfers between devices, local(): lax.ppermute(first, 'circ', [((i + 1) % ring, i) for i in range(ring)])  4.83 us
    ppermute x1, starting transfers between devices, local(): outer = lax.ppermute(outer, 'span', [(1, 2), (2, 1)])  4.26 us
    ppermute x1, starting transfers between devices, local(): inner = lax.ppermute(inner, 'span', [(0, 1), (1, 0), (2, 3), (3, 2)])  2.96 us
    pallas_call x1, Pallas kernels, local(): pl.pallas_call(section_kernel, out_shape=shape((640, 256), F32), in_specs...  2.82 us
    pallas_call x1, Pallas kernels, local(): pl.pallas_call(expand_kernel, out_shape=shape((64 * ROWS, 128), F32), in_...  2.4 us
    unnamed x9, local copies, waits for them, and re-layouts  1.74 us
  transfers between devices with their start and end apart: 5, of which 2 were waited for; matrix products, arithmetic and copies ran while one was open for 0% of the time, Pallas kernels for 0%

profile of v2, /device:TPU:1, one launch (start us, length us, event | category | flops | bytes accessed | tf_op | source)
XLA Modules:
  0.0 55.3 jit_solution(10514335011124975034)
XLA Ops:
  0.7 0.0 copy-start.2
  0.7 0.6 %copy-done.2 = s32[32]{0:T(128)S(1)} copy-done((s32[32]{0:T(128)S(1)}, s32[32]{0:T(128)}, u32[]{:S(2)}) %copy-start.2) | copy-done | bytes 152
  1.3 0.0 copy-start
  1.3 1.1 %copy-done = f32[65,5,4,64]{0,3,2,1:T(8,128)S(1)} copy-done((f32[65,5,4,64]{0,3,2,1:T(8,128)S(1)}, f32[65,5,4,64]{0,3,2,1:T(8,128)}, u32[]{:S(2)}) %copy-start) | copy-done | bytes 332824
  2.4 2.4 %expand.1 = f32[1280,128]{1,0:T(8,128)} custom-call(f32[1280,65]{1,0:T(8,128)S(1)} %bitcast.10, s32[1,32]{1,0:T(1,128)S(1)} %bitcast.12, s32[1]{0:T(128)S(6)} %copy.7.nodal_ref), custom_call_target="tpu_custom_call" | custom-call | tf_op jit(solution)/shard_map/expand/pallas_call | solution.py:120
  4.8 13.6 %all-to-all-start = ((f32[64,5,4,128]{3,2,1,0:T(4,128)}), f32[64,5,4,128]{3,2,1,0:T(4,128)S(1)}, u32[]{:S(2)}, u32[]{:S(2)}) async-start(f32[64,5,4,128]{3,2,1,0:T(4,128)} %bitcast.3), calls=%async_computation | async-start | bytes 1310720 | tf_op jit(solution)/shard_map/all_to_all | solution.py:128
  18.4 19.5 %all-to-all-done = f32[64,5,4,128]{3,2,1,0:T(4,128)S(1)} async-done(((f32[64,5,4,128]{3,2,1,0:T(4,128)}), f32[64,5,4,128]{3,2,1,0:T(4,128)S(1)}, u32[]{:S(2)}, u32[]{:S(2)}) %all-to-all-start) | async-done | bytes 655392 | tf_op jit(solution)/shard_map/all_to_all | solution.py:128
  37.9 0.0 copy-start.3
  37.9 0.0 copy-start.1
  37.9 0.3 gather.1
  38.2 3.0 %collective-permute-start = (f32[160,256]{1,0:T(8,128)S(1)}, f32[160,256]{1,0:T(8,128)S(1)}, u32[]{:S(2)}, u32[]{:S(2)}) collective-permute-start(f32[160,256]{1,0:T(8,128)S(1)} %get-tuple-element.11), channel_id=1, source_target_pairs={{0,1},{1,0},{2,3},{3,2},{4,5},{5,4},{6,7},{7,6},{8,9},{9,8},{10,11... | collective-permute-start | bytes 491528 | tf_op jit(solution)/shard_map/ppermute | solution.py:140
  41.2 4.3 %collective-permute-start.1 = (f32[160,256]{1,0:T(8,128)S(1)}, f32[160,256]{1,0:T(8,128)S(1)}, u32[]{:S(2)}, u32[]{:S(2)}) collective-permute-start(f32[160,256]{1,0:T(8,128)S(1)} %get-tuple-element.12), channel_id=1, source_target_pairs={{1,2},{2,1},{5,6},{6,5},{9,10},{10,9},{13,14},{14,13},{17,18},{18,... | collective-permute-start | bytes 491528 | tf_op jit(solution)/shard_map/ppermute | solution.py:137
  45.5 0.9 %collective-permute-start.2 = (f32[20,256]{1,0:T(8,128)S(1)}, f32[20,256]{1,0:T(8,128)S(1)}, u32[]{:S(2)}, u32[]{:S(2)}) collective-permute-start(f32[20,256]{1,0:T(8,128)S(1)} %get-tuple-element.13), channel_id=1, source_target_pairs={{0,4},{4,8},{8,12},{12,16},{16,20},{20,24},{24,28},{28,32},{32,36}... | collective-permute-start | bytes 61448 | tf_op jit(solution)/shard_map/ppermute | solution.py:138
  46.4 4.8 %collective-permute-start.3 = (f32[20,256]{1,0:T(8,128)S(1)}, f32[20,256]{1,0:T(8,128)S(1)}, u32[]{:S(2)}, u32[]{:S(2)}) collective-permute-start(f32[20,256]{1,0:T(8,128)S(1)} %get-tuple-element.14), channel_id=1, source_target_pairs={{4,0},{8,4},{12,8},{16,12},{20,16},{24,20},{28,24},{32,28},{36,32}... | collective-permute-start | bytes 61448 | tf_op jit(solution)/shard_map/ppermute | solution.py:139
  51.2 0.0 copy-done.3
  51.2 1.2 %collective-permute-done.2.before_ref = f32[20,256]{1,0:T(8,128)S(1)} collective-permute-done((f32[20,256]{1,0:T(8,128)S(1)}, f32[20,256]{1,0:T(8,128)S(1)}, u32[]{:S(2)}, u32[]{:S(2)}) %collective-permute-start.2) | collective-permute-done | bytes 20512 | tf_op jit(solution)/shard_map/ppermute | solution.py:138
  52.5 0.0 collective-permute-done.3.after_ref
  52.5 0.0 collective-permute-done.inner_ref
  52.5 0.0 collective-permute-done.1.outer_ref
  52.5 0.0 copy-done.1
  52.5 2.8 %section.1 = f32[640,256]{1,0:T(8,128)} custom-call(f32[640,256]{1,0:T(8,128)S(1)} %get-tuple-element.10.flow_ref, f32[160,256]{1,0:T(8,128)S(1)} %collective-permute-done.inner_ref, f32[160,256]{1,0:T(8,128)S(1)} %collective-permute-done.1.outer_ref, f32[20,256]{1,0:T(8,128)S(1)} %collective-permute-done.2.before_ref, ...), custom_call_target="tpu_custom_call" | custom-call | tf_op jit(solution)/shard_map/section/pallas_call | solution.py:141
  (1 shorter events, 0.0 us)
Async XLA Ops:
  0.7 0.7 %copy-start.2 = (s32[32]{0:T(128)S(1)}, s32[32]{0:T(128)}, u32[]{:S(2)}) copy-start(s32[32]{0:T(128)} %param.8) | copy-start | bytes 388
  1.3 1.1 %copy-start = (f32[65,5,4,64]{0,3,2,1:T(8,128)S(1)}, f32[65,5,4,64]{0,3,2,1:T(8,128)}, u32[]{:S(2)}) copy-start(f32[65,5,4,64]{0,3,2,1:T(8,128)} %param.5) | copy-start | bytes 998404
  4.8 33.1 %all-to-all-start = ((f32[64,5,4,128]{3,2,1,0:T(4,128)}), f32[64,5,4,128]{3,2,1,0:T(4,128)S(1)}, u32[]{:S(2)}, u32[]{:S(2)}) async-start(f32[64,5,4,128]{3,2,1,0:T(4,128)} %bitcast.3), calls=%async_computation | async-start | bytes 1310720 | tf_op jit(solution)/shard_map/all_to_all | solution.py:128
  37.9 13.3 %copy-start.3 = (f32[3,5,5]{2,0,1:T(4,128)S(1)}, f32[3,5,5]{2,0,1:T(4,128)}, u32[]{:S(2)}) copy-start(f32[3,5,5]{2,0,1:T(4,128)} %param.7) | copy-start | bytes 904
  37.9 14.5 %copy-start.1 = (f32[4,32,256]{2,1,0:T(8,128)S(1)}, f32[4,32,256]{2,1,0:T(8,128)}, u32[]{:S(2)}) copy-start(f32[4,32,256]{2,1,0:T(8,128)} %param.6) | copy-start | bytes 393220
  38.2 14.2 %collective-permute-start = (f32[160,256]{1,0:T(8,128)S(1)}, f32[160,256]{1,0:T(8,128)S(1)}, u32[]{:S(2)}, u32[]{:S(2)}) collective-permute-start(f32[160,256]{1,0:T(8,128)S(1)} %get-tuple-element.11), channel_id=1, source_target_pairs={{0,1},{1,0},{2,3},{3,2},{4,5},{5,4},{6,7},{7,6},{8,9},{9,8},{10,11... | collective-permute-start | bytes 491528 | tf_op jit(solution)/shard_map/ppermute | solution.py:140
  41.2 11.3 %collective-permute-start.1 = (f32[160,256]{1,0:T(8,128)S(1)}, f32[160,256]{1,0:T(8,128)S(1)}, u32[]{:S(2)}, u32[]{:S(2)}) collective-permute-start(f32[160,256]{1,0:T(8,128)S(1)} %get-tuple-element.12), channel_id=1, source_target_pairs={{1,2},{2,1},{5,6},{6,5},{9,10},{10,9},{13,14},{14,13},{17,18},{18,... | collective-permute-start | bytes 491528 | tf_op jit(solution)/shard_map/ppermute | solution.py:137
  45.5 7.0 %collective-permute-start.2 = (f32[20,256]{1,0:T(8,128)S(1)}, f32[20,256]{1,0:T(8,128)S(1)}, u32[]{:S(2)}, u32[]{:S(2)}) collective-permute-start(f32[20,256]{1,0:T(8,128)S(1)} %get-tuple-element.13), channel_id=1, source_target_pairs={{0,4},{4,8},{8,12},{12,16},{16,20},{20,24},{24,28},{28,32},{32,36}... | collective-permute-start | bytes 61448 | tf_op jit(solution)/shard_map/ppermute | solution.py:138
  46.4 6.0 %collective-permute-start.3 = (f32[20,256]{1,0:T(8,128)S(1)}, f32[20,256]{1,0:T(8,128)S(1)}, u32[]{:S(2)}, u32[]{:S(2)}) collective-permute-start(f32[20,256]{1,0:T(8,128)S(1)} %get-tuple-element.14), channel_id=1, source_target_pairs={{4,0},{8,4},{12,8},{16,12},{20,16},{24,20},{28,24},{32,28},{36,32}... | collective-permute-start | bytes 61448 | tf_op jit(solution)/shard_map/ppermute | solution.py:139

commit v3 on v2

v3 whole, which is shorter than its diff:
```python
import functools
import math

import jax
import jax.numpy as jnp
from jax import lax
from jax.experimental import pallas as pl
from jax.experimental.pallas import tpu as pltpu
from jax.sharding import PartitionSpec as P

VMEM = pl.BlockSpec(memory_space=pltpu.VMEM)
SMEM = pl.BlockSpec(memory_space=pltpu.SMEM)
F32 = jnp.float32
HBM = pl.BlockSpec(memory_space=pltpu.HBM)
ROWS = 20


def cos_turns(index):
    folded = jnp.where(index > 64, 128 - index, index)
    flip = folded > 32
    quarter = jnp.where(flip, 64 - folded, folded).astype(F32) * F32(math.pi / 64)
    square = quarter * quarter
    terms = [1.0, -1.0 / 2, 1.0 / 24, -1.0 / 720, 1.0 / 40320, -1.0 / 3628800, 1.0 / 479001600, -1.0 / 87178291200]
    value = jnp.full(index.shape, terms[-1], F32)
    for term in terms[-2::-1]:
        value = value * square + F32(term)
    return jnp.where(flip, -value, value)


def expand_kernel(coef_hbm, harm_hbm, nodal_hbm, out_ref, coef_ref, harm_ref, nodal_ref, sems):
    loads = [
        pltpu.make_async_copy(harm_hbm, harm_ref, sems.at[0]),
        pltpu.make_async_copy(nodal_hbm, nodal_ref, sems.at[1]),
        pltpu.make_async_copy(coef_hbm, coef_ref, sems.at[2]),
    ]
    for load in loads:
        load.start()
    lane = lax.broadcasted_iota(jnp.int32, (128, 128), 1)
    row = lax.broadcasted_iota(jnp.int32, (128, 128), 0)
    passage = jnp.where(row < 64, 2 * row, 2 * row - 127)
    loads[0].wait()
    loads[1].wait()
    harm = jnp.concatenate([harm_ref[...], jnp.zeros((1, 96), jnp.int32)], axis=1)
    turns = (pltpu.roll(harm, 1, 1) + pltpu.roll(harm, 33, 1)) * nodal_ref[...] & 127
    index = turns * passage & 127
    index = jnp.where(lane > 32, index + 96 & 127, index)
    phases = cos_turns(index)[:, :65]
    wide = phases.astype(jnp.bfloat16)
    rest = (phases - wide.astype(F32)).astype(jnp.bfloat16)
    product = functools.partial(
        lax.dot_general, dimension_numbers=(((1,), (1,)), ((), ())), preferred_element_type=F32
    )
    loads[2].wait()
    for group in range(5):
        values = coef_ref[group * 256 : group * 256 + 256, :]
        high = values.astype(jnp.bfloat16)
        low = (values - high.astype(F32)).astype(jnp.bfloat16)
        block = product(wide, high) + (product(wide, low) + product(rest, high))
        for h in range(2):
            pair = group * 2 + h
            cols = slice(128 * h, 128 * h + 128)
            out_ref[pl.ds(pair, 64, ROWS), :] = block[:64, cols]
            out_ref[pl.ds(pair + 10, 64, ROWS), :] = block[64:, cols]


def gather_kernel(got_ref, parity_ref, flow_ref, inner_ref, outer_ref, near_ref, far_ref):
    low = lax.broadcasted_iota(jnp.int32, (16, 128), 1) < 64
    even = parity_ref[0] == 0
    circ_even = parity_ref[1] == 0
    for p in range(2):
        for v in range(5):
            for h in range(2):
                row = p * 10 + v * 2 + h
                parts = [got_ref[pl.ds(a * ROWS + row, 16, 4 * ROWS), :] for a in range(4)]
                turned = [pltpu.roll(x, 64, 1) for x in parts]
                for b in range(2):
                    cols = slice(128 * b, 128 * b + 128)
                    base = (v * 4 + 2 * h) * 32 + p * 16
                    flow_ref[base : base + 16, cols] = jnp.where(low, parts[2 * b], turned[2 * b + 1])
                    flow_ref[base + 32 : base + 48, cols] = jnp.where(low, turned[2 * b], parts[2 * b + 1])
    for v in range(5):
        bottom = flow_ref[v * 128 : v * 128 + 32, :]
        top = flow_ref[v * 128 + 96 : v * 128 + 128, :]
        inner_ref[v * 32 : v * 32 + 32, :] = jnp.where(even, top, bottom)
        outer_ref[v * 32 : v * 32 + 32, :] = jnp.where(even, bottom, top)
    for i in range(20):
        first = flow_ref[i * 32 : i * 32 + 1, :]
        final = flow_ref[i * 32 + 31 : i * 32 + 32, :]
        near_ref[i : i + 1, :] = jnp.where(circ_even, final, first)
        far_ref[i : i + 1, :] = jnp.where(circ_even, first, final)


def halves(jac_ref, d):
    return [[0.5 * jac_ref[d, v, w] for w in range(5)] for v in range(5)]


def section_kernel(flow_ref, step_ref, jac_ref, part_ref):
    row = lax.broadcasted_iota(jnp.int32, (8, 256), 0)
    lane = lax.broadcasted_iota(jnp.int32, (8, 256), 1)
    at_top, at_bottom = row == 0, row == 7
    at_left, at_right = lane == 0, lane == 255
    half = [halves(jac_ref, d) for d in range(3)]
    for s in range(4):
        for t in range(4):
            diffs, smooth = [], []
            for v in range(5):
                base = (v * 4 + s) * 32 + t * 8
                here = flow_ref[base : base + 8, :]
                s_minus = flow_ref[base - 32 : base - 24, :] if s else jnp.zeros_like(here)
                s_plus = flow_ref[base + 32 : base + 40, :] if s < 3 else jnp.zeros_like(here)
                above = flow_ref[base - 1 : base, :] if t else 0.0
                below = flow_ref[base + 8 : base + 9, :] if t < 3 else 0.0
                p_minus = jnp.where(at_top, above, pltpu.roll(here, 1, 0))
                p_plus = jnp.where(at_bottom, below, pltpu.roll(here, 7, 0))
                a_minus = jnp.where(at_left, 0.0, pltpu.roll(here, 1, 1))
                a_plus = jnp.where(at_right, 0.0, pltpu.roll(here, 255, 1))
                diffs.append((s_plus - s_minus, p_plus - p_minus, a_plus - a_minus))
                total = (s_plus + s_minus) + (p_plus + p_minus) + (a_plus + a_minus)
                smooth.append((here, 0.75 * here - 0.125 * total))
            scale = 0.5 * step_ref[s * 32 + t * 8 : s * 32 + t * 8 + 8, :]
            for v in range(5):
                here, resid = smooth[v]
                for d in range(3):
                    for w in range(5):
                        resid = resid + half[d][v][w] * diffs[w][d]
                base = (v * 4 + s) * 32 + t * 8
                part_ref[base : base + 8, :] = here - scale * resid


def applied(half, sign, rows):
    out = []
    for v in range(5):
        total = -0.125 * rows[v]
        for w in range(5):
            total = total + (sign * half[v][w]) * rows[w]
        out.append(total)
    return out


def finish_kernel(part_ref, far_ref, outer_ref, near_ref, inner_ref, step_ref, jac_ref, parity_ref, out_ref):
    even = parity_ref[0] == 0
    circ_even = parity_ref[1] == 0
    half = halves(jac_ref, 0)
    for s in (0, 3):
        for t in range(4):
            rows = []
            for v in range(5):
                side = slice(v * 32 + t * 8, v * 32 + t * 8 + 8)
                inner, outer = inner_ref[side, :], outer_ref[side, :]
                rows.append(jnp.where(even, outer, inner) if s == 0 else jnp.where(even, inner, outer))
            scale = 0.5 * step_ref[s * 32 + t * 8 : s * 32 + t * 8 + 8, :]
            terms = applied(half, 1.0 if s else -1.0, rows)
            for v in range(5):
                base = (v * 4 + s) * 32 + t * 8
                out_ref[base : base + 8, :] = part_ref[base : base + 8, :] - scale * terms[v]
    for v in range(5):
        base = v * 128 + 32
        out_ref[base : base + 64, :] = part_ref[base : base + 64, :]
    half = halves(jac_ref, 1)
    for edge, sign in ((0, -1.0), (31, 1.0)):
        rows = []
        for v in range(5):
            near, far = near_ref[v * 4 : v * 4 + 4, :], far_ref[v * 4 : v * 4 + 4, :]
            rows.append(jnp.where(circ_even, near, far) if edge else jnp.where(circ_even, far, near))
        terms = applied(half, sign, rows)
        for s in range(4):
            scale = 0.5 * step_ref[s * 32 + edge : s * 32 + edge + 1, :]
            for v in range(5):
                at = (v * 4 + s) * 32 + edge
                out_ref[at : at + 1, :] = out_ref[at : at + 1, :] - scale * terms[v][s : s + 1, :]


def local(coefficients, local_step, jacobian, harmonic_numbers, nodal_diameter):
    shape = jax.ShapeDtypeStruct
    ring = lax.axis_size("circ")
    parity = jnp.stack([lax.axis_index("span") & 1, lax.axis_index("circ") & 1]).astype(jnp.int32)
    cells = coefficients.transpose(1, 2, 3, 0).reshape(1280, 65)
    params = pltpu.CompilerParams(vmem_limit_bytes=8 << 20)
    sent = pl.pallas_call(
        expand_kernel,
        out_shape=shape((64 * ROWS, 128), F32),
        in_specs=[HBM, HBM, HBM],
        out_specs=VMEM,
        scratch_shapes=[
            pltpu.VMEM((1280, 65), F32),
            pltpu.VMEM((1, 32), jnp.int32),
            pltpu.VMEM((1, 1), jnp.int32),
            pltpu.SemaphoreType.DMA((3,)),
        ],
        name="expand",
    )(cells, harmonic_numbers.reshape(1, 32), nodal_diameter.reshape(1, 1))
    got = lax.all_to_all(sent.reshape(64, 5, 4, 128), "circ", 0, 0, tiled=True).reshape(64 * ROWS, 128)
    sizes = [(640, 256), (160, 256), (160, 256), (20, 256), (20, 256)]
    flow, inner, outer, near, far = pl.pallas_call(
        gather_kernel,
        out_shape=[shape(size, F32) for size in sizes],
        in_specs=[VMEM, SMEM],
        out_specs=[VMEM] * 5,
        name="gather",
        compiler_params=params,
    )(got, parity)
    pairs = [(i, i + 1) for i in range(0, ring, 2)]
    between = [(i, (i + 1) % ring) for i in range(1, ring, 2)]
    far = lax.ppermute(far, "circ", between + [(j, i) for i, j in between])
    outer = lax.ppermute(outer, "span", [(1, 2), (2, 1)])
    near = lax.ppermute(near, "circ", pairs + [(j, i) for i, j in pairs])
    inner = lax.ppermute(inner, "span", [(0, 1), (1, 0), (2, 3), (3, 2)])
    step = local_step.reshape(128, 256)
    part = pl.pallas_call(
        section_kernel,
        out_shape=shape((640, 256), F32),
        in_specs=[VMEM, VMEM, SMEM],
        out_specs=VMEM,
        name="section",
        compiler_params=params,
        cost_estimate=pl.CostEstimate(flops=20_000_000, bytes_accessed=1_500_000, transcendentals=0),
    )(flow, step, jacobian)
    new = pl.pallas_call(
        finish_kernel,
        out_shape=shape((640, 256), F32),
        in_specs=[VMEM] * 6 + [SMEM] * 2,
        out_specs=VMEM,
        name="finish",
        compiler_params=params,
    )(part, far, outer, near, inner, step, jacobian, parity)
    return new.reshape(5, 4, 32, 256)


def solution(mesh):
    in_specs = (P(None, None, "span", "circ"), P("span", "circ", None), P(), P(), P())
    out_specs = P(None, "span", "circ", None)
    return jax.shard_map(local, mesh=mesh, in_specs=in_specs, out_specs=out_specs, check_vma=False)
```

time: 55.5 us -> 53.3 us (0.960)
  starting transfers between devices: 26.6 us -> 22.7 us
  waiting for transfers between devices: 20.8 us -> 22.7 us
  local copies, waits for them, and re-layouts: 1.74 us -> 0.01 us
  Pallas kernels: 5.53 us -> 7.03 us
    ppermute x2, starting transfers between devices: 5.76 us -> 1.87 us  [the longest x1 1.76 us: local(): far = lax.ppermute(far, 'circ', between + [(j, i) for i, j in between])]
    ppermute x1, starting transfers between devices: 2.96 us -> 0.09 us  [local(): inner = lax.ppermute(inner, 'span', [(0, 1), (1, 0), (2, 3), (3, 2)])]
    ppermute x1, starting transfers between devices: 4.26 us -> 7.11 us  [local(): outer = lax.ppermute(outer, 'span', [(1, 2), (2, 1)])]
    pallas_call x1 -> x2, Pallas kernels: 0.31 us -> 2.7 us  [the longest x1 1.86 us: local(): pl.pallas_call(finish_kernel, out_shape=shape((640, 256), F32), in_specs=...]
    ppermute x2, waiting for transfers between devices: 1.21 us -> 3.17 us  [the longest x1 3.17 us: local(): far = lax.ppermute(far, 'circ', between + [(j, i) for i, j in between])]
    unnamed x9 -> x5, local copies, waits for them, and re-layouts: 1.74 us -> 0.01 us
    pallas_call x1, Pallas kernels: 2.82 us -> 1.93 us  [local(): pl.pallas_call(section_kernel, out_shape=shape((640, 256), F32), in_specs...]
  transfers between devices with their start and end apart: 5 -> 5, of which waited for: 2 -> 2; matrix products, arithmetic and copies ran while one was open for 0% -> 0% of each run, Pallas kernels for 0% -> 4%
where the time goes in v3:
time: 53.3 us; the launch traced here: 53.1 us
  starting transfers between devices  22.7 us (43%)
  waiting for transfers between devices  22.7 us (43%)
  Pallas kernels  7.03 us (13%)
  between operations  0.7 us (1%)
    all_to_all x1, waiting for transfers between devices, local(): lax.all_to_all(sent.reshape(64, 5, 4, 128), 'circ', 0, 0, tiled=True)  19.5 us
    all_to_all x1, starting transfers between devices, local(): lax.all_to_all(sent.reshape(64, 5, 4, 128), 'circ', 0, 0, tiled=True)  13.6 us
    ppermute x1, starting transfers between devices, local(): outer = lax.ppermute(outer, 'span', [(1, 2), (2, 1)])  7.11 us
    ppermute x1, waiting for transfers between devices, local(): far = lax.ppermute(far, 'circ', between + [(j, i) for i, j in between])  3.17 us
    pallas_call x1, Pallas kernels, local(): pl.pallas_call(expand_kernel, out_shape=shape((64 * ROWS, 128), F32), in_...  2.4 us
    pallas_call x1, Pallas kernels, local(): pl.pallas_call(section_kernel, out_shape=shape((640, 256), F32), in_specs...  1.93 us
    pallas_call x1, Pallas kernels, local(): pl.pallas_call(finish_kernel, out_shape=shape((640, 256), F32), in_specs=...  1.86 us
    ppermute x1, starting transfers between devices, local(): far = lax.ppermute(far, 'circ', between + [(j, i) for i, j in between])  1.76 us
  transfers between devices with their start and end apart: 5, of which 2 were waited for; matrix products, arithmetic and copies ran while one was open for 0% of the time, Pallas kernels for 4%

profile of v3, /device:TPU:1, one launch (start us, length us, event | category | flops | bytes accessed | tf_op | source)
XLA Modules:
  0.0 53.1 jit_solution(14392503479778777828)
XLA Ops:
  0.7 2.4 %expand.1 = f32[1280,128]{1,0:T(8,128)} custom-call(f32[1280,65]{1,0:T(8,128)} %bitcast.16, s32[1,32]{1,0:T(1,128)} %bitcast.17, s32[1,1]{1,0:T(1,128)} %bitcast.11.nodal_hbm), custom_call_target="tpu_custom_call" | custom-call | tf_op jit(solution)/shard_map/expand/pallas_call | solution.py:179
  3.1 13.6 %all-to-all-start = ((f32[64,5,4,128]{3,2,1,0:T(4,128)}), f32[64,5,4,128]{3,2,1,0:T(4,128)S(1)}, u32[]{:S(2)}, u32[]{:S(2)}) async-start(f32[64,5,4,128]{3,2,1,0:T(4,128)} %bitcast.15), calls=%async_computation | async-start | bytes 1310720 | tf_op jit(solution)/shard_map/all_to_all | solution.py:192
  16.7 0.1 pad_add_fusion.parity_ref
  16.7 19.5 %all-to-all-done = f32[64,5,4,128]{3,2,1,0:T(4,128)S(1)} async-done(((f32[64,5,4,128]{3,2,1,0:T(4,128)}), f32[64,5,4,128]{3,2,1,0:T(4,128)S(1)}, u32[]{:S(2)}, u32[]{:S(2)}) %all-to-all-start) | async-done | bytes 655392 | tf_op jit(solution)/shard_map/all_to_all | solution.py:192
  36.2 0.0 copy-start.1
  36.2 0.0 copy-start
  36.2 0.8 %gather.1 = (f32[640,256]{1,0:T(8,128)S(1)}, f32[160,256]{1,0:T(8,128)S(1)}, f32[160,256]{1,0:T(8,128)S(1)}, f32[20,256]{1,0:T(8,128)S(1)}, f32[20,256]{1,0:T(8,128)S(1)}) custom-call(f32[1280,128]{1,0:T(8,128)S(1)} %bitcast.12, s32[2]{0:T(128)S(1)} %pad_add_fusion.parity_ref), custom_call_target="tpu_custom_call" | custom-call | tf_op jit(solution)/shard_map/gather/pallas_call | solution.py:194
  37.1 7.1 %collective-permute-start.1 = (f32[160,256]{1,0:T(8,128)S(1)}, f32[160,256]{1,0:T(8,128)S(1)}, u32[]{:S(2)}, u32[]{:S(2)}) collective-permute-start(f32[160,256]{1,0:T(8,128)S(1)} %get-tuple-element.12), channel_id=1, source_target_pairs={{1,2},{2,1},{5,6},{6,5},{9,10},{10,9},{13,14},{14,13},{17,18},{18,... | collective-permute-start | bytes 491528 | tf_op jit(solution)/shard_map/ppermute | solution.py:205
  44.2 0.1 collective-permute-start.3
  44.3 1.8 %collective-permute-start = (f32[20,256]{1,0:T(8,128)S(1)}, f32[20,256]{1,0:T(8,128)S(1)}, u32[]{:S(2)}, u32[]{:S(2)}) collective-permute-start(f32[20,256]{1,0:T(8,128)S(1)} %get-tuple-element.11), channel_id=1, source_target_pairs={{4,8},{12,16},{20,24},{28,32},{36,40},{44,48},{52,56},{60,64},{68,... | collective-permute-start | bytes 61448 | tf_op jit(solution)/shard_map/ppermute | solution.py:204
  46.0 0.1 collective-permute-start.2
  46.1 0.0 copy-done.1
  46.1 0.0 copy-done
  46.2 1.9 %section.1.part_ref = f32[640,256]{1,0:T(8,128)S(1)} custom-call(f32[640,256]{1,0:T(8,128)S(1)} %get-tuple-element.10.flow_ref, f32[128,256]{1,0:T(8,128)S(1)} %bitcast.13, f32[3,5,5]{2,1,0:T(8,128)S(1)} %copy.6.jac_ref), custom_call_target="tpu_custom_call" | custom-call | flops 20000000 | bytes 1500000 | tf_op jit(solution)/shard_map/section/pallas_call | solution.py:209
  48.1 3.2 %collective-permute-done.far_ref = f32[20,256]{1,0:T(8,128)S(1)} collective-permute-done((f32[20,256]{1,0:T(8,128)S(1)}, f32[20,256]{1,0:T(8,128)S(1)}, u32[]{:S(2)}, u32[]{:S(2)}) %collective-permute-start) | collective-permute-done | bytes 20512 | tf_op jit(solution)/shard_map/ppermute | solution.py:204
  51.3 0.0 collective-permute-done.2.near_ref
  51.3 0.0 collective-permute-done.1.outer_ref
  51.3 0.0 collective-permute-done.3.inner_ref
  51.3 1.9 %finish.1 = f32[640,256]{1,0:T(8,128)} custom-call(f32[640,256]{1,0:T(8,128)S(1)} %section.1.part_ref, f32[20,256]{1,0:T(8,128)S(1)} %collective-permute-done.far_ref, f32[160,256]{1,0:T(8,128)S(1)} %collective-permute-done.1.outer_ref, f32[20,256]{1,0:T(8,128)S(1)} %collective-permute-done.2.near_ref, f32[160,256]{1,0:T(8,128)S(1)} %collective-permute-done.3.inner_ref, ...), custom_call_target="tpu_custom_call" | custom-call | tf_op jit(solution)/shard_map/finish/pallas_call | solution.py:218
  (1 shorter events, 0.0 us)
Async XLA Ops:
  3.1 33.2 %all-to-all-start = ((f32[64,5,4,128]{3,2,1,0:T(4,128)}), f32[64,5,4,128]{3,2,1,0:T(4,128)S(1)}, u32[]{:S(2)}, u32[]{:S(2)}) async-start(f32[64,5,4,128]{3,2,1,0:T(4,128)} %bitcast.15), calls=%async_computation | async-start | bytes 1310720 | tf_op jit(solution)/shard_map/all_to_all | solution.py:192
  36.2 9.9 %copy-start.1 = (f32[3,5,5]{2,0,1:T(4,128)S(1)}, f32[3,5,5]{2,0,1:T(4,128)}, u32[]{:S(2)}) copy-start(f32[3,5,5]{2,0,1:T(4,128)} %param.7) | copy-start | bytes 904
  36.2 9.9 %copy-start = (f32[4,32,256]{2,1,0:T(8,128)S(1)}, f32[4,32,256]{2,1,0:T(8,128)}, u32[]{:S(2)}) copy-start(f32[4,32,256]{2,1,0:T(8,128)} %param.6) | copy-start | bytes 393220
  37.1 14.2 %collective-permute-start.1 = (f32[160,256]{1,0:T(8,128)S(1)}, f32[160,256]{1,0:T(8,128)S(1)}, u32[]{:S(2)}, u32[]{:S(2)}) collective-permute-start(f32[160,256]{1,0:T(8,128)S(1)} %get-tuple-element.12), channel_id=1, source_target_pairs={{1,2},{2,1},{5,6},{6,5},{9,10},{10,9},{13,14},{14,13},{17,18},{18,... | collective-permute-start | bytes 491528 | tf_op jit(solution)/shard_map/ppermute | solution.py:205
  44.2 7.1 %collective-permute-start.3 = (f32[160,256]{1,0:T(8,128)S(1)}, f32[160,256]{1,0:T(8,128)S(1)}, u32[]{:S(2)}, u32[]{:S(2)}) collective-permute-start(f32[160,256]{1,0:T(8,128)S(1)} %get-tuple-element.14), channel_id=1, source_target_pairs={{0,1},{1,0},{2,3},{3,2},{4,5},{5,4},{6,7},{7,6},{8,9},{9,8},{10,11... | collective-permute-start | bytes 491528 | tf_op jit(solution)/shard_map/ppermute | solution.py:207
  44.3 7.0 %collective-permute-start = (f32[20,256]{1,0:T(8,128)S(1)}, f32[20,256]{1,0:T(8,128)S(1)}, u32[]{:S(2)}, u32[]{:S(2)}) collective-permute-start(f32[20,256]{1,0:T(8,128)S(1)} %get-tuple-element.11), channel_id=1, source_target_pairs={{4,8},{12,16},{20,24},{28,32},{36,40},{44,48},{52,56},{60,64},{68,... | collective-permute-start | bytes 61448 | tf_op jit(solution)/shard_map/ppermute | solution.py:204
  46.0 5.2 %collective-permute-start.2 = (f32[20,256]{1,0:T(8,128)S(1)}, f32[20,256]{1,0:T(8,128)S(1)}, u32[]{:S(2)}, u32[]{:S(2)}) collective-permute-start(f32[20,256]{1,0:T(8,128)S(1)} %get-tuple-element.13), channel_id=1, source_target_pairs={{0,4},{8,12},{16,20},{24,28},{32,36},{40,44},{48,52},{56,60},{64,6... | collective-permute-start | bytes 61448 | tf_op jit(solution)/shard_map/ppermute | solution.py:206

commit v4 on v3

--- a/solution.py
+++ b/solution.py
@@ -41,7 +41,7 @@
     loads[0].wait()
     loads[1].wait()
     harm = jnp.concatenate([harm_ref[...], jnp.zeros((1, 96), jnp.int32)], axis=1)
-    turns = (pltpu.roll(harm, 1, 1) + pltpu.roll(harm, 33, 1)) * nodal_ref[...] & 127
+    turns = (pltpu.roll(harm, 1, 1) + pltpu.roll(harm, 33, 1)) * nodal_ref[0] & 127
     index = turns * passage & 127
     index = jnp.where(lane > 32, index + 96 & 127, index)
     phases = cos_turns(index)[:, :65]
@@ -65,8 +65,6 @@
 
 def gather_kernel(got_ref, parity_ref, flow_ref, inner_ref, outer_ref, near_ref, far_ref):
     low = lax.broadcasted_iota(jnp.int32, (16, 128), 1) < 64
-    even = parity_ref[0] == 0
-    circ_even = parity_ref[1] == 0
     for p in range(2):
         for v in range(5):
             for h in range(2):
@@ -78,16 +76,15 @@
                     base = (v * 4 + 2 * h) * 32 + p * 16
                     flow_ref[base : base + 16, cols] = jnp.where(low, parts[2 * b], turned[2 * b + 1])
                     flow_ref[base + 32 : base + 48, cols] = jnp.where(low, turned[2 * b], parts[2 * b + 1])
-    for v in range(5):
-        bottom = flow_ref[v * 128 : v * 128 + 32, :]
-        top = flow_ref[v * 128 + 96 : v * 128 + 128, :]
-        inner_ref[v * 32 : v * 32 + 32, :] = jnp.where(even, top, bottom)
-        outer_ref[v * 32 : v * 32 + 32, :] = jnp.where(even, bottom, top)
+    layer, row = parity_ref[0] * 96, parity_ref[1] * 31
+    for v in range(5):
+        inner_at = pl.multiple_of(v * 128 + 96 - layer, 32)
+        outer_at = pl.multiple_of(v * 128 + layer, 32)
+        inner_ref[v * 32 : v * 32 + 32, :] = flow_ref[pl.ds(inner_at, 32), :]
+        outer_ref[v * 32 : v * 32 + 32, :] = flow_ref[pl.ds(outer_at, 32), :]
     for i in range(20):
-        first = flow_ref[i * 32 : i * 32 + 1, :]
-        final = flow_ref[i * 32 + 31 : i * 32 + 32, :]
-        near_ref[i : i + 1, :] = jnp.where(circ_even, final, first)
-        far_ref[i : i + 1, :] = jnp.where(circ_even, first, final)
+        near_ref[i : i + 1, :] = flow_ref[pl.ds(i * 32 + 31 - row, 1), :]
+        far_ref[i : i + 1, :] = flow_ref[pl.ds(i * 32 + row, 1), :]
 
 
 def halves(jac_ref, d):
@@ -127,47 +124,50 @@
                 part_ref[base : base + 8, :] = here - scale * resid
 
 
-def applied(half, sign, rows):
+def applied(half, rows):
     out = []
     for v in range(5):
         total = -0.125 * rows[v]
         for w in range(5):
-            total = total + (sign * half[v][w]) * rows[w]
+            total = total + half[v][w] * rows[w]
         out.append(total)
     return out
 
 
-def finish_kernel(part_ref, far_ref, outer_ref, near_ref, inner_ref, step_ref, jac_ref, parity_ref, out_ref):
-    even = parity_ref[0] == 0
-    circ_even = parity_ref[1] == 0
+def finish_kernel(part_ref, far_ref, outer_ref, near_ref, inner_ref, step_ref, jac_ref, parity_ref, out_hbm, new_ref, sem):
+    layer, row = parity_ref[0], parity_ref[1]
+    half = halves(jac_ref, 1)
+    for v in range(5):
+        new_ref[v * 128 : v * 128 + 128, :] = part_ref[v * 128 : v * 128 + 128, :]
+    for edge_ref, edge in ((near_ref, 1 - row), (far_ref, row)):
+        sign = 2.0 * edge.astype(F32) - 1.0
+        terms = applied([[sign * x for x in line] for line in half], [edge_ref[v * 4 : v * 4 + 4, :] for v in range(5)])
+        for s in range(4):
+            scale = 0.5 * step_ref[pl.ds(s * 32 + 31 * edge, 1), :]
+            for v in range(5):
+                at = pl.ds((v * 4 + s) * 32 + 31 * edge, 1)
+                new_ref[at, :] = part_ref[at, :] - scale * terms[v][s : s + 1, :]
+    copies = []
+    for v in range(5):
+        rows = slice(v * 128 + 32, v * 128 + 96)
+        copies.append(pltpu.make_async_copy(new_ref.at[rows, :], out_hbm.at[rows, :], sem.at[v]))
+        copies[-1].start()
     half = halves(jac_ref, 0)
-    for s in (0, 3):
+    for i, (side_ref, side) in enumerate(((inner_ref, 1 - layer), (outer_ref, layer))):
+        sign = 2.0 * side.astype(F32) - 1.0
+        signed = [[sign * x for x in line] for line in half]
         for t in range(4):
-            rows = []
-            for v in range(5):
-                side = slice(v * 32 + t * 8, v * 32 + t * 8 + 8)
-                inner, outer = inner_ref[side, :], outer_ref[side, :]
-                rows.append(jnp.where(even, outer, inner) if s == 0 else jnp.where(even, inner, outer))
-            scale = 0.5 * step_ref[s * 32 + t * 8 : s * 32 + t * 8 + 8, :]
-            terms = applied(half, 1.0 if s else -1.0, rows)
-            for v in range(5):
-                base = (v * 4 + s) * 32 + t * 8
-                out_ref[base : base + 8, :] = part_ref[base : base + 8, :] - scale * terms[v]
-    for v in range(5):
-        base = v * 128 + 32
-        out_ref[base : base + 64, :] = part_ref[base : base + 64, :]
-    half = halves(jac_ref, 1)
-    for edge, sign in ((0, -1.0), (31, 1.0)):
-        rows = []
+            terms = applied(signed, [side_ref[v * 32 + t * 8 : v * 32 + t * 8 + 8, :] for v in range(5)])
+            scale = 0.5 * step_ref[pl.ds(pl.multiple_of(side * 96 + t * 8, 8), 8), :]
+            for v in range(5):
+                at = pl.ds(pl.multiple_of(v * 128 + side * 96 + t * 8, 8), 8)
+                new_ref[at, :] = new_ref[at, :] - scale * terms[v]
         for v in range(5):
-            near, far = near_ref[v * 4 : v * 4 + 4, :], far_ref[v * 4 : v * 4 + 4, :]
-            rows.append(jnp.where(circ_even, near, far) if edge else jnp.where(circ_even, far, near))
-        terms = applied(half, sign, rows)
-        for s in range(4):
-            scale = 0.5 * step_ref[s * 32 + edge : s * 32 + edge + 1, :]
-            for v in range(5):
-                at = (v * 4 + s) * 32 + edge
-                out_ref[at : at + 1, :] = out_ref[at : at + 1, :] - scale * terms[v][s : s + 1, :]
+            rows = pl.ds(pl.multiple_of(v * 128 + side * 96, 32), 32)
+            copies.append(pltpu.make_async_copy(new_ref.at[rows, :], out_hbm.at[rows, :], sem.at[5 + 5 * i + v]))
+            copies[-1].start()
+    for copy in copies:
+        copy.wait()
 
 
 def local(coefficients, local_step, jacobian, harmonic_numbers, nodal_diameter):
@@ -184,11 +184,11 @@
         scratch_shapes=[
             pltpu.VMEM((1280, 65), F32),
             pltpu.VMEM((1, 32), jnp.int32),
-            pltpu.VMEM((1, 1), jnp.int32),
+            pltpu.SMEM((1,), jnp.int32),
             pltpu.SemaphoreType.DMA((3,)),
         ],
         name="expand",
-    )(cells, harmonic_numbers.reshape(1, 32), nodal_diameter.reshape(1, 1))
+    )(cells, harmonic_numbers.reshape(1, 32), nodal_diameter)
     got = lax.all_to_all(sent.reshape(64, 5, 4, 128), "circ", 0, 0, tiled=True).reshape(64 * ROWS, 128)
     sizes = [(640, 256), (160, 256), (160, 256), (20, 256), (20, 256)]
     flow, inner, outer, near, far = pl.pallas_call(
@@ -219,7 +219,8 @@
         finish_kernel,
         out_shape=shape((640, 256), F32),
         in_specs=[VMEM] * 6 + [SMEM] * 2,
-        out_specs=VMEM,
+        out_specs=HBM,
+        scratch_shapes=[pltpu.VMEM((640, 256), F32), pltpu.SemaphoreType.DMA((15,))],
         name="finish",
         compiler_params=params,
     )(part, far, outer, near, inner, step, jacobian, parity)

time: 53.3 us -> 53.4 us (level)
  no operation moved by 1% of the time
where the time goes in v4:
time: 53.4 us; the launch traced here: 53.2 us
  starting transfers between devices  22.7 us (43%)
  waiting for transfers between devices  22.7 us (43%)
  Pallas kernels  7.1 us (13%)
  between operations  0.71 us (1%)
    all_to_all x1, waiting for transfers between devices, local(): lax.all_to_all(sent.reshape(64, 5, 4, 128), 'circ', 0, 0, tiled=True)  19.5 us
    all_to_all x1, starting transfers between devices, local(): lax.all_to_all(sent.reshape(64, 5, 4, 128), 'circ', 0, 0, tiled=True)  13.6 us
    ppermute x1, starting transfers between devices, local(): outer = lax.ppermute(outer, 'span', [(1, 2), (2, 1)])  7.11 us
    ppermute x1, waiting for transfers between devices, local(): far = lax.ppermute(far, 'circ', between + [(j, i) for i, j in between])  3.17 us
    pallas_call x1, Pallas kernels, local(): pl.pallas_call(expand_kernel, out_shape=shape((64 * ROWS, 128), F32), in_...  2.4 us
    pallas_call x1, Pallas kernels, local(): pl.pallas_call(section_kernel, out_shape=shape((640, 256), F32), in_specs...  1.93 us
    pallas_call x1, Pallas kernels, local(): pl.pallas_call(finish_kernel, out_shape=shape((640, 256), F32), in_specs=...  1.9 us
    ppermute x1, starting transfers between devices, local(): far = lax.ppermute(far, 'circ', between + [(j, i) for i, j in between])  1.76 us
  transfers between devices with their start and end apart: 5, of which 2 were waited for; matrix products, arithmetic and copies ran while one was open for 0% of the time, Pallas kernels for 4%

profile of v4, /device:TPU:1, one launch (start us, length us, event | category | flops | bytes accessed | tf_op | source)
XLA Modules:
  0.0 53.2 jit_solution(5553951820238855291)
XLA Ops:
  0.7 2.4 %expand.1 = f32[1280,128]{1,0:T(8,128)} custom-call(f32[1280,65]{1,0:T(8,128)} %bitcast.14, s32[1,32]{1,0:T(1,128)} %bitcast.15, s32[1]{0:T(128)S(6)} %copy.8.nodal_hbm), custom_call_target="tpu_custom_call" | custom-call | tf_op jit(solution)/shard_map/expand/pallas_call | solution.py:179
  3.1 13.6 %all-to-all-start = ((f32[64,5,4,128]{3,2,1,0:T(4,128)}), f32[64,5,4,128]{3,2,1,0:T(4,128)S(1)}, u32[]{:S(2)}, u32[]{:S(2)}) async-start(f32[64,5,4,128]{3,2,1,0:T(4,128)} %bitcast.13), calls=%async_computation | async-start | bytes 1310720 | tf_op jit(solution)/shard_map/all_to_all | solution.py:192
  16.7 0.1 pad_add_fusion.parity_ref
  16.7 19.5 %all-to-all-done = f32[64,5,4,128]{3,2,1,0:T(4,128)S(1)} async-done(((f32[64,5,4,128]{3,2,1,0:T(4,128)}), f32[64,5,4,128]{3,2,1,0:T(4,128)S(1)}, u32[]{:S(2)}, u32[]{:S(2)}) %all-to-all-start) | async-done | bytes 655392 | tf_op jit(solution)/shard_map/all_to_all | solution.py:192
  36.2 0.0 copy-start.1
  36.2 0.0 copy-start
  36.2 0.9 %gather.1 = (f32[640,256]{1,0:T(8,128)S(1)}, f32[160,256]{1,0:T(8,128)S(1)}, f32[160,256]{1,0:T(8,128)S(1)}, f32[20,256]{1,0:T(8,128)S(1)}, f32[20,256]{1,0:T(8,128)S(1)}) custom-call(f32[1280,128]{1,0:T(8,128)S(1)} %bitcast.10, s32[2]{0:T(128)S(1)} %pad_add_fusion.parity_ref), custom_call_target="tpu_custom_call" | custom-call | tf_op jit(solution)/shard_map/gather/pallas_call | solution.py:194
  37.1 7.1 %collective-permute-start.1 = (f32[160,256]{1,0:T(8,128)S(1)}, f32[160,256]{1,0:T(8,128)S(1)}, u32[]{:S(2)}, u32[]{:S(2)}) collective-permute-start(f32[160,256]{1,0:T(8,128)S(1)} %get-tuple-element.12), channel_id=1, source_target_pairs={{1,2},{2,1},{5,6},{6,5},{9,10},{10,9},{13,14},{14,13},{17,18},{18,... | collective-permute-start | bytes 491528 | tf_op jit(solution)/shard_map/ppermute | solution.py:205
  44.2 0.1 collective-permute-start.3
  44.3 1.8 %collective-permute-start = (f32[20,256]{1,0:T(8,128)S(1)}, f32[20,256]{1,0:T(8,128)S(1)}, u32[]{:S(2)}, u32[]{:S(2)}) collective-permute-start(f32[20,256]{1,0:T(8,128)S(1)} %get-tuple-element.11), channel_id=1, source_target_pairs={{4,8},{12,16},{20,24},{28,32},{36,40},{44,48},{52,56},{60,64},{68,... | collective-permute-start | bytes 61448 | tf_op jit(solution)/shard_map/ppermute | solution.py:204
  46.1 0.1 collective-permute-start.2
  46.2 0.0 copy-done.1
  46.2 0.0 copy-done
  46.2 1.9 %section.1.part_ref = f32[640,256]{1,0:T(8,128)S(1)} custom-call(f32[640,256]{1,0:T(8,128)S(1)} %get-tuple-element.10.flow_ref, f32[128,256]{1,0:T(8,128)S(1)} %bitcast.11, f32[3,5,5]{2,1,0:T(8,128)S(1)} %copy.6.jac_ref), custom_call_target="tpu_custom_call" | custom-call | flops 20000000 | bytes 1500000 | tf_op jit(solution)/shard_map/section/pallas_call | solution.py:209
  48.1 3.2 %collective-permute-done.far_ref = f32[20,256]{1,0:T(8,128)S(1)} collective-permute-done((f32[20,256]{1,0:T(8,128)S(1)}, f32[20,256]{1,0:T(8,128)S(1)}, u32[]{:S(2)}, u32[]{:S(2)}) %collective-permute-start) | collective-permute-done | bytes 20512 | tf_op jit(solution)/shard_map/ppermute | solution.py:204
  51.3 0.0 collective-permute-done.2.near_ref
  51.3 0.0 collective-permute-done.1.outer_ref
  51.3 0.0 collective-permute-done.3.inner_ref
  51.3 1.9 %finish.1 = f32[640,256]{1,0:T(8,128)} custom-call(f32[640,256]{1,0:T(8,128)S(1)} %section.1.part_ref, f32[20,256]{1,0:T(8,128)S(1)} %collective-permute-done.far_ref, f32[160,256]{1,0:T(8,128)S(1)} %collective-permute-done.1.outer_ref, f32[20,256]{1,0:T(8,128)S(1)} %collective-permute-done.2.near_ref, f32[160,256]{1,0:T(8,128)S(1)} %collective-permute-done.3.inner_ref, ...), custom_call_target="tpu_custom_call" | custom-call | tf_op jit(solution)/shard_map/finish/pallas_call | solution.py:218
  (1 shorter events, 0.0 us)
Async XLA Ops:
  3.1 33.2 %all-to-all-start = ((f32[64,5,4,128]{3,2,1,0:T(4,128)}), f32[64,5,4,128]{3,2,1,0:T(4,128)S(1)}, u32[]{:S(2)}, u32[]{:S(2)}) async-start(f32[64,5,4,128]{3,2,1,0:T(4,128)} %bitcast.13), calls=%async_computation | async-start | bytes 1310720 | tf_op jit(solution)/shard_map/all_to_all | solution.py:192
  36.2 10.0 %copy-start.1 = (f32[3,5,5]{2,0,1:T(4,128)S(1)}, f32[3,5,5]{2,0,1:T(4,128)}, u32[]{:S(2)}) copy-start(f32[3,5,5]{2,0,1:T(4,128)} %param.7) | copy-start | bytes 904
  36.2 10.0 %copy-start = (f32[4,32,256]{2,1,0:T(8,128)S(1)}, f32[4,32,256]{2,1,0:T(8,128)}, u32[]{:S(2)}) copy-start(f32[4,32,256]{2,1,0:T(8,128)} %param.6) | copy-start | bytes 393220
  37.1 14.2 %collective-permute-start.1 = (f32[160,256]{1,0:T(8,128)S(1)}, f32[160,256]{1,0:T(8,128)S(1)}, u32[]{:S(2)}, u32[]{:S(2)}) collective-permute-start(f32[160,256]{1,0:T(8,128)S(1)} %get-tuple-element.12), channel_id=1, source_target_pairs={{1,2},{2,1},{5,6},{6,5},{9,10},{10,9},{13,14},{14,13},{17,18},{18,... | collective-permute-start | bytes 491528 | tf_op jit(solution)/shard_map/ppermute | solution.py:205
  44.2 7.1 %collective-permute-start.3 = (f32[160,256]{1,0:T(8,128)S(1)}, f32[160,256]{1,0:T(8,128)S(1)}, u32[]{:S(2)}, u32[]{:S(2)}) collective-permute-start(f32[160,256]{1,0:T(8,128)S(1)} %get-tuple-element.14), channel_id=1, source_target_pairs={{0,1},{1,0},{2,3},{3,2},{4,5},{5,4},{6,7},{7,6},{8,9},{9,8},{10,11... | collective-permute-start | bytes 491528 | tf_op jit(solution)/shard_map/ppermute | solution.py:207
  44.3 7.0 %collective-permute-start = (f32[20,256]{1,0:T(8,128)S(1)}, f32[20,256]{1,0:T(8,128)S(1)}, u32[]{:S(2)}, u32[]{:S(2)}) collective-permute-start(f32[20,256]{1,0:T(8,128)S(1)} %get-tuple-element.11), channel_id=1, source_target_pairs={{4,8},{12,16},{20,24},{28,32},{36,40},{44,48},{52,56},{60,64},{68,... | collective-permute-start | bytes 61448 | tf_op jit(solution)/shard_map/ppermute | solution.py:204
  46.1 5.2 %collective-permute-start.2 = (f32[20,256]{1,0:T(8,128)S(1)}, f32[20,256]{1,0:T(8,128)S(1)}, u32[]{:S(2)}, u32[]{:S(2)}) collective-permute-start(f32[20,256]{1,0:T(8,128)S(1)} %get-tuple-element.13), channel_id=1, source_target_pairs={{0,4},{8,12},{16,20},{24,28},{32,36},{40,44},{48,52},{56,60},{64,6... | collective-permute-start | bytes 61448 | tf_op jit(solution)/shard_map/ppermute | solution.py:206

commit v5 on v4

v5 whole, which is shorter than its diff:
```python
import functools
import math

import jax
import jax.numpy as jnp
from jax import lax
from jax.experimental import pallas as pl
from jax.experimental.pallas import tpu as pltpu
from jax.sharding import PartitionSpec as P

VMEM = pl.BlockSpec(memory_space=pltpu.VMEM)
SMEM = pl.BlockSpec(memory_space=pltpu.SMEM)
HBM = pl.BlockSpec(memory_space=pltpu.HBM)
F32 = jnp.float32
ROWS = 20
LAYERS = ((0, 3), (1, 2))


def cos_turns(index):
    folded = jnp.where(index > 64, 128 - index, index)
    flip = folded > 32
    quarter = jnp.where(flip, 64 - folded, folded).astype(F32) * F32(math.pi / 64)
    square = quarter * quarter
    terms = [1.0, -1.0 / 2, 1.0 / 24, -1.0 / 720, 1.0 / 40320, -1.0 / 3628800, 1.0 / 479001600, -1.0 / 87178291200]
    value = jnp.full(index.shape, terms[-1], F32)
    for term in terms[-2::-1]:
        value = value * square + F32(term)
    return jnp.where(flip, -value, value)


def expand_kernel(coef_hbm, harm_hbm, nodal_ref, out_ref, coef_ref, harm_ref, sems):
    loads = [
        pltpu.make_async_copy(harm_hbm, harm_ref, sems.at[0]),
        pltpu.make_async_copy(coef_hbm, coef_ref, sems.at[1]),
    ]
    for load in loads:
        load.start()
    lane = lax.broadcasted_iota(jnp.int32, (128, 128), 1)
    row = lax.broadcasted_iota(jnp.int32, (128, 128), 0)
    passage = jnp.where(row < 64, 2 * row, 2 * row - 127)
    loads[0].wait()
    harm = jnp.concatenate([harm_ref[...], jnp.zeros((1, 96), jnp.int32)], axis=1)
    turns = (pltpu.roll(harm, 1, 1) + pltpu.roll(harm, 33, 1)) * nodal_ref[0] & 127
    index = turns * passage & 127
    index = jnp.where(lane > 32, index + 96 & 127, index)
    phases = cos_turns(index)[:, :65]
    wide = phases.astype(jnp.bfloat16)
    rest = (phases - wide.astype(F32)).astype(jnp.bfloat16)
    product = functools.partial(
        lax.dot_general, dimension_numbers=(((1,), (1,)), ((), ())), preferred_element_type=F32
    )
    loads[1].wait()
    for v in range(5):
        values = jnp.concatenate([coef_ref[pl.ds((v * 4 + s) * 64, 64), :] for s in (0, 3, 1, 2)], axis=0)
        high = values.astype(jnp.bfloat16)
        low = (values - high.astype(F32)).astype(jnp.bfloat16)
        block = product(wide, high) + (product(wide, low) + product(rest, high))
        for p in range(2):
            for m in range(2):
                out_ref[pl.ds(p * 10 + m * 5 + v, 64, ROWS), :] = block[p * 64 : p * 64 + 64, m * 128 : m * 128 + 128]


def paired(parts):
    low = lax.broadcasted_iota(jnp.int32, parts[0].shape, 1) < 64
    turned = [pltpu.roll(x, 64, 1) for x in parts]
    lower = [jnp.where(low, parts[2 * b], turned[2 * b + 1]) for b in range(2)]
    upper = [jnp.where(low, turned[2 * b], parts[2 * b + 1]) for b in range(2)]
    return lower, upper


def edges_kernel(got_ref, far_ref, outer_ref, near_ref, inner_ref, first_ref, final_ref):
    even, circ_even = (lax.axis_index(axis) & 1 == 0 for axis in ("span", "circ"))
    for rim_ref, source, passage in ((first_ref, 0, 0), (final_ref, 60, 1)):
        for m in range(2):
            start = passage * 10 + m * 5
            both = paired([got_ref[pl.ds((source + a) * ROWS + start, 5), :] for a in range(4)])
            for s, halves_of in zip(LAYERS[m], both):
                for b in range(2):
                    rim_ref[pl.ds(b * 20 + s, 5, 4), :] = halves_of[b]
    first, final = first_ref[...], final_ref[...]
    near_ref[...] = jnp.where(circ_even, final, first)
    far_ref[...] = jnp.where(circ_even, first, final)
    for p in range(2):
        for v in range(5):
            bottom, top = paired([got_ref[pl.ds(a * ROWS + p * 10 + v, 16, 4 * ROWS), :] for a in range(4)])
            rows = slice(v * 32 + p * 16, v * 32 + p * 16 + 16)
            for b in range(2):
                cols = slice(128 * b, 128 * b + 128)
                inner_ref[rows, cols] = jnp.where(even, top[b], bottom[b])
                outer_ref[rows, cols] = jnp.where(even, bottom[b], top[b])


def prepare_kernel(step_ref, jac_ref, scale_ref, half_ref):
    scale_ref[...] = 0.5 * step_ref[...]
    for d in range(3):
        for v in range(5):
            for w in range(5):
                row = (d * 5 + v) * 5 + w
                half_ref[row : row + 1, :] = jnp.full((1, 128), 0.5 * jac_ref[d, v, w], F32)


def weighted(half_ref, d, v, w, values):
    row = (d * 5 + v) * 5 + w
    line = half_ref[row : row + 1, :]
    return jnp.concatenate([line] * (values.shape[1] // 128), axis=1) * values


def section_kernel(got_ref, scale_ref, half_ref, part_ref, flow_ref):
    for v in range(5):
        for p in range(2):
            for m in range(2):
                row = p * 10 + m * 5 + v
                parts = [got_ref[pl.ds(a * ROWS + row, 16, 4 * ROWS), :] for a in range(4)]
                for s, halves_of in zip(LAYERS[m], paired(parts)):
                    base = (v * 4 + s) * 32 + p * 16
                    for b in range(2):
                        flow_ref[base : base + 16, 128 * b : 128 * b + 128] = halves_of[b]
    row = lax.broadcasted_iota(jnp.int32, (8, 256), 0)
    lane = lax.broadcasted_iota(jnp.int32, (8, 256), 1)
    at_top, at_bottom = row == 0, row == 7
    at_left, at_right = lane == 0, lane == 255
    for s in range(4):
        for t in range(4):
            diffs, smooth = [], []
            for v in range(5):
                base = (v * 4 + s) * 32 + t * 8
                here = flow_ref[base : base + 8, :]
                s_minus = flow_ref[base - 32 : base - 24, :] if s else jnp.zeros_like(here)
                s_plus = flow_ref[base + 32 : base + 40, :] if s < 3 else jnp.zeros_like(here)
                above = flow_ref[base - 1 : base, :] if t else 0.0
                below = flow_ref[base + 8 : base + 9, :] if t < 3 else 0.0
                p_minus = jnp.where(at_top, above, pltpu.roll(here, 1, 0))
                p_plus = jnp.where(at_bottom, below, pltpu.roll(here, 7, 0))
                a_minus = jnp.where(at_left, 0.0, pltpu.roll(here, 1, 1))
                a_plus = jnp.where(at_right, 0.0, pltpu.roll(here, 255, 1))
                diffs.append((s_plus - s_minus, p_plus - p_minus, a_plus - a_minus))
                total = (s_plus + s_minus) + (p_plus + p_minus) + (a_plus + a_minus)
                smooth.append((here, 0.75 * here - 0.125 * total))
            scale = scale_ref[s * 32 + t * 8 : s * 32 + t * 8 + 8, :]
            for v in range(5):
                here, resid = smooth[v]
                for d in range(3):
                    for w in range(5):
                        resid = resid + weighted(half_ref, d, v, w, diffs[w][d])
                base = (v * 4 + s) * 32 + t * 8
                part_ref[base : base + 8, :] = here - scale * resid


def applied(half_ref, d, sign, rows):
    out = []
    for v in range(5):
        total = -0.125 * rows[v]
        for w in range(5):
            term = weighted(half_ref, d, v, w, rows[w])
            total = total + term if sign > 0 else total - term
        out.append(total)
    return out


def finish_kernel(part_ref, far_ref, outer_ref, near_ref, inner_ref, scale_ref, half_ref, out_hbm, new_ref, sem):
    even, circ_even = (lax.axis_index(axis) & 1 == 0 for axis in ("span", "circ"))
    near, far = near_ref[...], far_ref[...]
    for v in range(5):
        new_ref[v * 128 : v * 128 + 128, :] = part_ref[v * 128 : v * 128 + 128, :]
    for edge, sign, rim in ((0, -1, jnp.where(circ_even, far, near)), (31, 1, jnp.where(circ_even, near, far))):
        for b in range(2):
            cols = slice(128 * b, 128 * b + 128)
            terms = applied(half_ref, 1, sign, [rim[b * 20 + v * 4 : b * 20 + v * 4 + 4] for v in range(5)])
            for s in range(4):
                scale = scale_ref[s * 32 + edge : s * 32 + edge + 1, cols]
                for v in range(5):
                    at = (v * 4 + s) * 32 + edge
                    new_ref[at : at + 1, cols] = part_ref[at : at + 1, cols] - scale * terms[v][s : s + 1]
    copies = []
    for v in range(5):
        rows = slice(v * 128 + 32, v * 128 + 96)
        copies.append(pltpu.make_async_copy(new_ref.at[rows, :], out_hbm.at[rows, :], sem.at[v]))
        copies[-1].start()
    for i, s in enumerate((0, 3)):
        for t in range(4):
            rows = []
            for v in range(5):
                side = slice(v * 32 + t * 8, v * 32 + t * 8 + 8)
                inner, outer = inner_ref[side, :], outer_ref[side, :]
                rows.append(jnp.where(even, inner, outer) if s else jnp.where(even, outer, inner))
            terms = applied(half_ref, 0, 1 if s else -1, rows)
            scale = scale_ref[s * 32 + t * 8 : s * 32 + t * 8 + 8, :]
            for v in range(5):
                at = slice((v * 4 + s) * 32 + t * 8, (v * 4 + s) * 32 + t * 8 + 8)
                new_ref[at, :] = new_ref[at, :] - scale * terms[v]
        for v in range(5):
            rows = slice((v * 4 + s) * 32, (v * 4 + s) * 32 + 32)
            copies.append(pltpu.make_async_copy(new_ref.at[rows, :], out_hbm.at[rows, :], sem.at[5 + 5 * i + v]))
            copies[-1].start()
    for copy in copies:
        copy.wait()


def local(coefficients, local_step, jacobian, harmonic_numbers, nodal_diameter):
    shape = jax.ShapeDtypeStruct
    ring = lax.axis_size("circ")
    cells = coefficients.transpose(1, 2, 3, 0).reshape(1280, 65)
    params = pltpu.CompilerParams(vmem_limit_bytes=8 << 20)
    sent = pl.pallas_call(
        expand_kernel,
        out_shape=shape((64 * ROWS, 128), F32),
        in_specs=[HBM, HBM, SMEM],
        out_specs=VMEM,
        scratch_shapes=[
            pltpu.VMEM((1280, 65), F32),
            pltpu.VMEM((1, 32), jnp.int32),
            pltpu.SemaphoreType.DMA((2,)),
        ],
        name="expand",
    )(cells, harmonic_numbers.reshape(1, 32), nodal_diameter)
    pairs = [(i, i + 1) for i in range(0, ring, 2)]
    between = [(i, (i + 1) % ring) for i in range(1, ring, 2)]
    got = lax.all_to_all(sent.reshape(64, 5, 4, 128), "circ", 0, 0, tiled=True)
    got = got.reshape(64 * ROWS, 128)
    scale, half = pl.pallas_call(
        prepare_kernel,
        out_shape=[shape((128, 256), F32), shape((80, 128), F32)],
        in_specs=[VMEM, SMEM],
        out_specs=[VMEM, VMEM],
        name="prepare",
        compiler_params=params,
    )(local_step.reshape(128, 256), jacobian)
    sizes = [(40, 128), (160, 256), (40, 128), (160, 256)]
    far, outer, near, inner = pl.pallas_call(
        edges_kernel,
        out_shape=[shape(size, F32) for size in sizes],
        in_specs=[VMEM],
        out_specs=[VMEM] * 4,
        scratch_shapes=[pltpu.VMEM((40, 128), F32)] * 2,
        name="edges",
        compiler_params=params,
    )(got)
    far = lax.ppermute(far, "circ", between + [(j, i) for i, j in between])
    outer = lax.ppermute(outer, "span", [(1, 2), (2, 1)])
    near = lax.ppermute(near, "circ", pairs + [(j, i) for i, j in pairs])
    inner = lax.ppermute(inner, "span", [(0, 1), (1, 0), (2, 3), (3, 2)])
    part = pl.pallas_call(
        section_kernel,
        out_shape=shape((640, 256), F32),
        in_specs=[VMEM] * 3,
        out_specs=VMEM,
        scratch_shapes=[pltpu.VMEM((640, 256), F32)],
        name="section",
        compiler_params=params,
        cost_estimate=pl.CostEstimate(flops=20_000_000, bytes_accessed=1_500_000, transcendentals=0),
    )(got, scale, half)
    new = pl.pallas_call(
        finish_kernel,
        out_shape=shape((640, 256), F32),
        in_specs=[VMEM] * 7,
        out_specs=HBM,
        scratch_shapes=[pltpu.VMEM((640, 256), F32), pltpu.SemaphoreType.DMA((15,))],
        name="finish",
        compiler_params=params,
    )(part, far, outer, near, inner, scale, half)
    return new.reshape(5, 4, 32, 256)


def solution(mesh):
    in_specs = (P(None, None, "span", "circ"), P("span", "circ", None), P(), P(), P())
    out_specs = P(None, "span", "circ", None)
    return jax.shard_map(local, mesh=mesh, in_specs=in_specs, out_specs=out_specs, check_vma=False)
```

time: 53.4 us -> 51.8 us (0.970)
  blocking collectives: 0 us -> 33.1 us
  waiting for transfers between devices: 22.7 us -> 2.86 us
  starting transfers between devices: 22.7 us -> 9.08 us
  Pallas kernels: 7.1 us -> 5.84 us
    all_to_all x0 -> x1, blocking collectives: none -> 33.1 us  [local(): got = lax.all_to_all(sent.reshape(64, 5, 4, 128), 'circ', 0, 0, tiled=True)]
    all_to_all x1 -> x0, waiting for transfers between devices: 19.5 us -> none  [local(): lax.all_to_all(sent.reshape(64, 5, 4, 128), 'circ', 0, 0, tiled=True)]
    all_to_all x1 -> x0, starting transfers between devices: 13.6 us -> none  [local(): lax.all_to_all(sent.reshape(64, 5, 4, 128), 'circ', 0, 0, tiled=True)]
    pallas_call x1, Pallas kernels: 1.9 us -> 1.08 us  [local(): pl.pallas_call(finish_kernel, out_shape=shape((640, 256), F32), in_specs=...]
  transfers between devices with their start and end apart: 5 -> 4, of which waited for: 2 -> 1; matrix products, arithmetic and copies ran while one was open for 0% -> 0% of each run, Pallas kernels for 4% -> 4%
where the time goes in v5:
time: 51.8 us; the launch traced here: 51.6 us
  blocking collectives  33.1 us (64%)
  starting transfers between devices  9.08 us (18%)
  Pallas kernels  5.84 us (11%)
  waiting for transfers between devices  2.86 us (6%)
  between operations  0.7 us (1%)
    all_to_all x1, blocking collectives, local(): got = lax.all_to_all(sent.reshape(64, 5, 4, 128), 'circ', 0, 0, tiled=True)  33.1 us
    ppermute x1, starting transfers between devices, local(): outer = lax.ppermute(outer, 'span', [(1, 2), (2, 1)])  7.12 us
    ppermute x1, waiting for transfers between devices, local(): far = lax.ppermute(far, 'circ', between + [(j, i) for i, j in between])  2.85 us
    pallas_call x1, Pallas kernels, local(): pl.pallas_call(expand_kernel, out_shape=shape((64 * ROWS, 128), F32), in_...  2.39 us
    ppermute x1, starting transfers between devices, local(): far = lax.ppermute(far, 'circ', between + [(j, i) for i, j in between])  1.76 us
    pallas_call x1, Pallas kernels, local(): pl.pallas_call(section_kernel, out_shape=shape((640, 256), F32), in_specs...  1.41 us
    pallas_call x1, Pallas kernels, local(): pl.pallas_call(finish_kernel, out_shape=shape((640, 256), F32), in_specs=...  1.08 us
  transfers between devices with their start and end apart: 4, of which 1 were waited for; matrix products, arithmetic and copies ran while one was open for 0% of the time, Pallas kernels for 4%

profile of v5, /device:TPU:1, one launch (start us, length us, event | category | flops | bytes accessed | tf_op | source)
XLA Modules:
  0.0 51.6 jit_solution(18046455446511446897)
XLA Ops:
  0.7 2.4 %expand.1 = f32[1280,128]{1,0:T(8,128)} custom-call(f32[1280,65]{1,0:T(8,128)} %bitcast.12, s32[1,32]{1,0:T(1,128)} %bitcast.13, s32[1]{0:T(128)S(6)} %copy.7.nodal_ref), custom_call_target="tpu_custom_call" | custom-call | tf_op jit(solution)/shard_map/expand/pallas_call | solution.py:204
  3.0 33.1 %all_to_all.5 = f32[64,5,4,128]{3,2,1,0:T(4,128)S(1)} all-to-all(f32[64,5,4,128]{3,2,1,0:T(4,128)} %bitcast.11), channel_id=1, replica_groups=mesh['circ'=64,'span'=4] {'circ'}, dimensions={0} | all-to-all | bytes 1310720 | tf_op jit(solution)/shard_map/all_to_all | solution.py:218
  36.2 0.0 copy-start.1
  36.2 0.0 copy-start
  36.2 0.2 edges.1
  36.4 7.1 %collective-permute-start.1 = (f32[160,256]{1,0:T(8,128)S(1)}, f32[160,256]{1,0:T(8,128)S(1)}, u32[]{:S(2)}, u32[]{:S(2)}) collective-permute-start(f32[160,256]{1,0:T(8,128)S(1)} %get-tuple-element.14), channel_id=1, source_target_pairs={{1,2},{2,1},{5,6},{6,5},{9,10},{10,9},{13,14},{14,13},{17,18},{18,... | collective-permute-start | bytes 491528 | tf_op jit(solution)/shard_map/ppermute | solution.py:239
  43.5 0.1 collective-permute-start.3
  43.6 1.8 %collective-permute-start = (f32[40,128]{1,0:T(8,128)S(1)}, f32[40,128]{1,0:T(8,128)S(1)}, u32[]{:S(2)}, u32[]{:S(2)}) collective-permute-start(f32[40,128]{1,0:T(8,128)S(1)} %get-tuple-element.13), channel_id=1, source_target_pairs={{4,8},{12,16},{20,24},{28,32},{36,40},{44,48},{52,56},{60,64},{68,... | collective-permute-start | bytes 61448 | tf_op jit(solution)/shard_map/ppermute | solution.py:238
  45.4 0.1 collective-permute-start.2
  45.5 0.0 copy-done.1
  45.5 0.0 copy-done
  45.5 0.8 %prepare.1 = (f32[128,256]{1,0:T(8,128)S(1)}, f32[80,128]{1,0:T(8,128)S(1)}) custom-call(f32[128,256]{1,0:T(8,128)S(1)} %bitcast.10, f32[3,5,5]{2,1,0:T(8,128)S(1)} %copy.6.jac_ref), custom_call_target="tpu_custom_call" | custom-call | tf_op jit(solution)/shard_map/prepare/pallas_call | solution.py:220
  46.3 1.4 %section.1.part_ref = f32[640,256]{1,0:T(8,128)S(1)} custom-call(f32[1280,128]{1,0:T(8,128)S(1)} %bitcast.9, f32[128,256]{1,0:T(8,128)S(1)} %get-tuple-element.11.scale_ref, f32[80,128]{1,0:T(8,128)S(1)} %get-tuple-element.12.half_ref), custom_call_target="tpu_custom_call" | custom-call | flops 20000000 | bytes 1500000 | tf_op jit(solution)/shard_map/section/pallas_call | solution.py:242
  47.7 2.9 %collective-permute-done.far_ref = f32[40,128]{1,0:T(8,128)S(1)} collective-permute-done((f32[40,128]{1,0:T(8,128)S(1)}, f32[40,128]{1,0:T(8,128)S(1)}, u32[]{:S(2)}, u32[]{:S(2)}) %collective-permute-start) | collective-permute-done | bytes 20512 | tf_op jit(solution)/shard_map/ppermute | solution.py:238
  50.5 0.0 collective-permute-done.2.near_ref
  50.5 0.0 collective-permute-done.1.outer_ref
  50.5 0.0 collective-permute-done.3.inner_ref
  50.5 1.1 %finish.1 = f32[640,256]{1,0:T(8,128)} custom-call(f32[640,256]{1,0:T(8,128)S(1)} %section.1.part_ref, f32[40,128]{1,0:T(8,128)S(1)} %collective-permute-done.far_ref, f32[160,256]{1,0:T(8,128)S(1)} %collective-permute-done.1.outer_ref, f32[40,128]{1,0:T(8,128)S(1)} %collective-permute-done.2.near_ref, f32[160,256]{1,0:T(8,128)S(1)} %collective-permute-done.3.inner_ref, ...), custom_call_target="tpu_custom_call" | custom-call | tf_op jit(solution)/shard_map/finish/pallas_call | solution.py:252
  (1 shorter events, 0.0 us)
Async XLA Ops:
  36.2 9.3 %copy-start.1 = (f32[3,5,5]{2,0,1:T(4,128)S(1)}, f32[3,5,5]{2,0,1:T(4,128)}, u32[]{:S(2)}) copy-start(f32[3,5,5]{2,0,1:T(4,128)} %param.7) | copy-start | bytes 904
  36.2 9.3 %copy-start = (f32[4,32,256]{2,1,0:T(8,128)S(1)}, f32[4,32,256]{2,1,0:T(8,128)}, u32[]{:S(2)}) copy-start(f32[4,32,256]{2,1,0:T(8,128)} %param.6) | copy-start | bytes 393220
  36.4 14.2 %collective-permute-start.1 = (f32[160,256]{1,0:T(8,128)S(1)}, f32[160,256]{1,0:T(8,128)S(1)}, u32[]{:S(2)}, u32[]{:S(2)}) collective-permute-start(f32[160,256]{1,0:T(8,128)S(1)} %get-tuple-element.14), channel_id=1, source_target_pairs={{1,2},{2,1},{5,6},{6,5},{9,10},{10,9},{13,14},{14,13},{17,18},{18,... | collective-permute-start | bytes 491528 | tf_op jit(solution)/shard_map/ppermute | solution.py:239
  43.5 7.0 %collective-permute-start.3 = (f32[160,256]{1,0:T(8,128)S(1)}, f32[160,256]{1,0:T(8,128)S(1)}, u32[]{:S(2)}, u32[]{:S(2)}) collective-permute-start(f32[160,256]{1,0:T(8,128)S(1)} %get-tuple-element.16), channel_id=1, source_target_pairs={{0,1},{1,0},{2,3},{3,2},{4,5},{5,4},{6,7},{7,6},{8,9},{9,8},{10,11... | collective-permute-start | bytes 491528 | tf_op jit(solution)/shard_map/ppermute | solution.py:241
  43.6 6.9 %collective-permute-start = (f32[40,128]{1,0:T(8,128)S(1)}, f32[40,128]{1,0:T(8,128)S(1)}, u32[]{:S(2)}, u32[]{:S(2)}) collective-permute-start(f32[40,128]{1,0:T(8,128)S(1)} %get-tuple-element.13), channel_id=1, source_target_pairs={{4,8},{12,16},{20,24},{28,32},{36,40},{44,48},{52,56},{60,64},{68,... | collective-permute-start | bytes 61448 | tf_op jit(solution)/shard_map/ppermute | solution.py:238
  45.4 5.2 %collective-permute-start.2 = (f32[40,128]{1,0:T(8,128)S(1)}, f32[40,128]{1,0:T(8,128)S(1)}, u32[]{:S(2)}, u32[]{:S(2)}) collective-permute-start(f32[40,128]{1,0:T(8,128)S(1)} %get-tuple-element.15), channel_id=1, source_target_pairs={{0,4},{8,12},{16,20},{24,28},{32,36},{40,44},{48,52},{56,60},{64,6... | collective-permute-start | bytes 61448 | tf_op jit(solution)/shard_map/ppermute | solution.py:240
